TPU v7x, 32 devices: a whole 2x2x4 slice. The times are simulated.
32 devices in a mesh: row: 4 (over y, core), col: 8 (over z, x).
Axes of the slice: x: 2, y: 2, z: 4, core: 2. Of those that a mesh axis runs over, the one named last changes fastest.
Arguments:
- grads: bfloat16 [1024, 8192], P('row', 'col'), may hold values from -64 to 64
Outputs:
- kernel: float32 [1024, 1024], P('row', 'col')
All inputs are finite; a program needn't handle non-finite values.
Results may differ from a plain program's by a relative error of at most 0.002.
Values may be sent and summed in bfloat16 or wider, within the bound.
No kernel may reach another device: no remote copies, remote signals or barrier semaphores. Data moves between devices by JAX's collectives and lax.ppermute only.
A program may use at most 64 MiB of HBM per device.

v0:
```python
import functools

import jax
import jax.numpy as jnp
from jax import lax
from jax.experimental import pallas as pl
from jax.experimental.pallas import tpu as pltpu
from jax.sharding import PartitionSpec as P

BW = 64
LANES = 128
SUB = 8
VMEM_LIMIT = 16 << 20


def lane_gather(rows, index):
    return jnp.take_along_axis(rows, index, axis=1, mode="promise_in_bounds")


def gram(x):
    return lax.dot_general(x, x, (((0,), (0,)), ((), ())), preferred_element_type=jnp.float32)


def times(x, y):
    return lax.dot_general(x, y, (((1,), (0,)), ((), ())), preferred_element_type=jnp.float32)


def times_transposed(x, y):
    return lax.dot_general(x, y, (((1,), (1,)), ((), ())), preferred_element_type=jnp.float32)


def fisher_sums(grads, store):
    width = grads[0].shape[1]
    wide = min(2 * LANES, width)
    low = lax.broadcasted_iota(jnp.int32, (BW, LANES), 1) < BW
    for w in range(width // wide):
        x = jnp.concatenate([g[:, w * wide : (w + 1) * wide] for g in grads], axis=0)
        square = gram(x)
        for h in range(wide // LANES):
            at = h * LANES
            tile = square[at : at + LANES, at : at + LANES]
            store(w * (wide // LANES) + h, jnp.where(low, tile[:BW], tile[BW:]))


def broadcast_row(block, i):
    return jnp.broadcast_to(block[i : i + 1, :], block.shape)


def to_lanes(packed, rows, groups):
    low = lax.broadcasted_iota(jnp.int32, (BW, LANES), 1) < BW
    for lo in range(SUB):
        parts = []
        for hi in range(BW // SUB):
            part = packed[pl.ds(hi * SUB + lo, groups, stride=BW), :]
            parts += [part] * (SUB // groups)
        half = jnp.concatenate(parts, axis=0)
        turned = jnp.concatenate([half, half], axis=0).T
        rows[pl.ds(lo, BW, stride=SUB), :] = jnp.where(low, turned[:BW], turned[BW:])


def from_lanes(rows, inverse, groups):
    lane = lax.broadcasted_iota(jnp.int32, (LANES, LANES), 1)
    sub = lax.broadcasted_iota(jnp.int32, (LANES, LANES), 0)
    same = (lane < BW) == (sub < BW)
    for lo in range(SUB):
        half = rows[pl.ds(lo, BW, stride=SUB), :]
        turned = jnp.where(same, jnp.concatenate([half, half], axis=0).T, 0.0)
        for h in range(LANES // BW):
            for hi in range(BW // SUB):
                at = (h * (BW // SUB) + hi) * SUB
                inverse[pl.ds(h * BW + hi * SUB + lo, groups, stride=LANES), :] = turned[
                    at : at + groups
                ]


def factor(rows):
    lane = lax.broadcasted_iota(jnp.int32, (SUB, LANES), 1)
    sub = lax.broadcasted_iota(jnp.int32, (SUB, LANES), 0)
    chunk = (lane // SUB) % (BW // SUB)
    column = chunk * SUB + sub
    base = (lane // BW) * BW + lane % SUB

    def at(k):
        return slice(k * SUB, (k + 1) * SUB)

    for p in range(BW // SUB):
        first = p * SUB
        panel = [rows[at(first + q), :] for q in range(SUB)]
        near = [lane_gather(row, base + first) for row in panel]
        inside = chunk == p
        steps = []
        for q in range(SUB):
            here = column == first + q
            pivot = broadcast_row(near[q], q)
            inv = 1.0 / pivot
            step = jnp.where(here, 1.0, panel[q]) * inv
            near_step = near[q] * inv
            for k in range(q + 1, SUB):
                down = broadcast_row(near[q], k)
                panel[k] = jnp.where(here, 0.0, panel[k]) - down * step
                near[k] = near[k] - down * near_step
            steps.append(jnp.where(jnp.logical_and(inside, sub > q), 0.0, step))
            rows[at(first + q), :] = jnp.where(
                column < first + q, panel[q], jnp.where(here, 1.0, 0.0)
            ) * lax.rsqrt(pivot)
        for hi in range(p + 1, BW // SUB):
            downs = [lane_gather(row, base + hi * SUB) for row in panel]
            for lo in range(SUB):
                k = hi * SUB + lo
                row = jnp.where(inside, 0.0, rows[at(k), :])
                for q in range(SUB):
                    row = row - broadcast_row(downs[q], lo) * steps[q]
                rows[at(k), :] = row


def early_body(*refs):
    *grads, sums = refs

    def store(s, value):
        sums[s] = value

    fisher_sums(grads, store)


def body(sums_ref, *refs, slots, peers, total):
    grads = refs[:slots]
    outs = refs[slots : slots + peers]
    packed, rows, inverse, white = refs[slots + peers :]
    count, width = grads[0].shape
    block = outs[0].shape[1]
    groups = width // LANES

    lane = lax.broadcasted_iota(jnp.int32, (BW, LANES), 1)
    sub = lax.broadcasted_iota(jnp.int32, (BW, LANES), 0)
    unit = jnp.where(sub == lane % BW, 0.1, 0.0)

    def store(s, value):
        packed[s * BW : (s + 1) * BW, :] = (sums_ref[s] + value) * (1.0 / total) + unit

    fisher_sums(grads[slots // 2 :], store)
    to_lanes(packed, rows, groups)
    factor(rows)
    from_lanes(rows, inverse, groups)

    wide = min(2 * LANES, width)
    pairs = wide // LANES
    zero = jnp.zeros((LANES, LANES), jnp.float32)
    for w in range(width // wide):
        blocks = []
        for h in range(pairs):
            s = w * pairs + h
            tile = inverse[s * LANES : (s + 1) * LANES, :]
            blocks.append(jnp.concatenate([tile if i == h else zero for i in range(pairs)], axis=1))
        matrix = jnp.concatenate(blocks, axis=0)
        high = matrix.astype(jnp.bfloat16)
        rest = (matrix - high.astype(jnp.float32)).astype(jnp.bfloat16)
        for t in range(slots):
            x = grads[t][:, w * wide : (w + 1) * wide]
            out = (times(x, high) + times(x, rest)).astype(jnp.bfloat16)
            for h in range(pairs):
                white[w * pairs + h, t * count : (t + 1) * count, :] = out[
                    :, h * LANES : (h + 1) * LANES
                ]

    row = lax.axis_index("row")
    col = lax.axis_index("col")
    per_slot = count // block

    def white_rows(start, size):
        return jnp.concatenate(
            [white[s, pl.ds(start, size), :] for s in range(width // LANES)], axis=1
        )

    mine = white_rows(0, count)
    for first in range(0, peers, 2):
        stacked = []
        for p in (first, first + 1):
            peer = col ^ p
            start = ((peer // per_slot) ^ row) * count + (peer % per_slot) * block
            stacked.append(white_rows(pl.multiple_of(start, block), block))
        out = times_transposed(mine, jnp.concatenate(stacked, axis=0))
        for i in range(2):
            outs[first + i][...] = out[:, i * block : (i + 1) * block].astype(
                outs[first + i].dtype
            )


def per_device(grads):
    slots = lax.axis_size("row")
    peers = lax.axis_size("col")
    count, width = grads.shape
    total = count * slots
    block = total // peers
    groups = width // LANES
    vmem = pl.BlockSpec(memory_space=pltpu.VMEM)
    params = pltpu.CompilerParams(vmem_limit_bytes=VMEM_LIMIT)

    def swap(x, bit):
        return lax.ppermute(x, "row", [(i, i ^ bit) for i in range(slots)])

    far = slots // 2
    held = {0: grads, far: swap(grads, far)}
    bit = far // 2
    while bit:
        for t in list(held):
            held[t ^ bit] = swap(held[t], bit)
        bit //= 2

    near = [held[t] for t in range(far)]
    sums = pl.pallas_call(
        early_body,
        in_specs=[vmem] * far,
        out_specs=vmem,
        out_shape=jax.ShapeDtypeStruct((groups, BW, LANES), jnp.float32),
        compiler_params=params,
    )(*near)

    outs = pl.pallas_call(
        functools.partial(body, slots=slots, peers=peers, total=total),
        in_specs=[vmem] * (slots + 1),
        out_specs=[vmem] * peers,
        out_shape=[
            jax.ShapeDtypeStruct((count, block), jnp.bfloat16 if p else jnp.float32)
            for p in range(peers)
        ],
        scratch_shapes=[
            pltpu.VMEM((groups * BW, LANES), jnp.float32),
            pltpu.VMEM((BW * SUB, LANES), jnp.float32),
            pltpu.VMEM((groups * LANES, LANES), jnp.float32),
            pltpu.VMEM((groups, total, LANES), jnp.bfloat16),
        ],
        compiler_params=params,
    )(sums, *[held[t] for t in range(slots)])

    got = [
        lax.ppermute(outs[p], "col", [(i, i ^ p) for i in range(peers)])
        for p in reversed(range(1, peers))
    ]
    kernel = outs[0]
    for part in got:
        kernel = kernel + part.astype(jnp.float32)
    return kernel * (width * peers) ** (-0.5)


def solution(mesh):
    return jax.shard_map(
        per_device,
        mesh=mesh,
        in_specs=(P("row", "col"),),
        out_specs=P("row", "col"),
        check_vma=False,
    )
```

profile of v0, /device:TPU:0, one launch (start us, length us, event | category | flops | bytes accessed | tf_op | source)
XLA Modules:
  0.0 39.7 jit_solution(7536402289726315253)
XLA Ops:
  0.0 3.0 %collective-permute-start.1 = (bf16[256,1024]{1,0:T(8,128)(2,1)}, bf16[256,1024]{1,0:T(8,128)(2,1)S(1)}, u32[]{:S(2)}, u32[]{:S(2)}) collective-permute-start(bf16[256,1024]{1,0:T(8,128)(2,1)} %refs_0_.3), channel_id=1, source_target_pairs={{0,16},{8,24},{16,0},{24,8},{1,17},{9,25},{17,1},{25,9},{2,18},{10... | collective-permute-start | bytes 1572872 | tf_op jit(solution)/shard_map/ppermute | solution.py:199
  3.0 0.0 collective-permute-start
  3.0 12.1 %collective-permute-done.1.refs_2_ = bf16[256,1024]{1,0:T(8,128)(2,1)S(1)} collective-permute-done((bf16[256,1024]{1,0:T(8,128)(2,1)}, bf16[256,1024]{1,0:T(8,128)(2,1)S(1)}, u32[]{:S(2)}, u32[]{:S(2)}) %collective-permute-start.1) | collective-permute-done | bytes 524320 | tf_op jit(solution)/shard_map/ppermute | solution.py:199
  15.1 0.0 collective-permute-start.2
  15.1 0.0 collective-permute-done.refs_1_
  15.1 0.0 copy-start
  15.1 1.0 %copy-done = bf16[256,1024]{1,0:T(8,128)(2,1)S(1)} copy-done((bf16[256,1024]{1,0:T(8,128)(2,1)S(1)}, bf16[256,1024]{1,0:T(8,128)(2,1)}, u32[]{:S(2)}) %copy-start) | copy-done | bytes 524312
  16.2 0.0 copy-start.1
  16.2 0.5 %shard_map.17.sums_ref = f32[8,64,128]{2,1,0:T(8,128)S(1)} custom-call(bf16[256,1024]{1,0:T(8,128)(2,1)S(1)} %copy-done, bf16[256,1024]{1,0:T(8,128)(2,1)S(1)} %collective-permute-done.refs_1_), custom_call_target="tpu_custom_call" | custom-call | tf_op jit(solution)/shard_map/pallas_call | solution.py:210
  16.7 0.4 collective-permute-done.2.refs_3_
  17.0 0.2 copy-done.1
  17.2 4.9 %shard_map.18 = (f32[256,128]{1,0:T(8,128)S(1)}, bf16[256,128]{1,0:T(8,128)(2,1)S(1)}, bf16[256,128]{1,0:T(8,128)(2,1)S(1)}, bf16[256,128]{1,0:T(8,128)(2,1)S(1)...) custom-call(f32[8,64,128]{2,1,0:T(8,128)S(1)} %shard_map.17.sums_ref, ...), custom_call_target="tpu_custom_call" | custom-call | tf_op jit(solution)/shard_map/pallas_call | solution.py:218
  22.1 4.8 %collective-permute-start.3 = (bf16[256,128]{1,0:T(8,128)(2,1)S(1)}, bf16[256,128]{1,0:T(8,128)(2,1)S(1)}, u32[]{:S(2)}, u32[]{:S(2)}) collective-permute-start(bf16[256,128]{1,0:T(8,128)(2,1)S(1)} %get-tuple-element.14), channel_id=1, source_target_pairs={{0,7},{1,6},{2,5},{3,4},{4,3},{5,2},{6,1},{7,0},{8,15},{9,14},{10,... | collective-permute-start | bytes 196616 | tf_op jit(solution)/shard_map/ppermute | solution.py:236
  26.9 0.2 collective-permute-start.4
  27.2 0.8 %collective-permute-start.5 = (bf16[256,128]{1,0:T(8,128)(2,1)S(1)}, bf16[256,128]{1,0:T(8,128)(2,1)S(1)}, u32[]{:S(2)}, u32[]{:S(2)}) collective-permute-start(bf16[256,128]{1,0:T(8,128)(2,1)S(1)} %get-tuple-element.16), channel_id=1, source_target_pairs={{0,5},{1,4},{2,7},{3,6},{4,1},{5,0},{6,3},{7,2},{8,13},{9,12},{10,... | collective-permute-start | bytes 196616 | tf_op jit(solution)/shard_map/ppermute | solution.py:236
  27.9 2.0 %collective-permute-start.6 = (bf16[256,128]{1,0:T(8,128)(2,1)S(1)}, bf16[256,128]{1,0:T(8,128)(2,1)S(1)}, u32[]{:S(2)}, u32[]{:S(2)}) collective-permute-start(bf16[256,128]{1,0:T(8,128)(2,1)S(1)} %get-tuple-element.17), channel_id=1, source_target_pairs={{0,4},{1,5},{2,6},{3,7},{4,0},{5,1},{6,2},{7,3},{8,12},{9,13},{10,... | collective-permute-start | bytes 196616 | tf_op jit(solution)/shard_map/ppermute | solution.py:236
  30.0 2.3 %collective-permute-start.7 = (bf16[256,128]{1,0:T(8,128)(2,1)S(1)}, bf16[256,128]{1,0:T(8,128)(2,1)S(1)}, u32[]{:S(2)}, u32[]{:S(2)}) collective-permute-start(bf16[256,128]{1,0:T(8,128)(2,1)S(1)} %get-tuple-element.18), channel_id=1, source_target_pairs={{0,3},{1,2},{2,1},{3,0},{4,7},{5,6},{6,5},{7,4},{8,11},{9,10},{10,... | collective-permute-start | bytes 196616 | tf_op jit(solution)/shard_map/ppermute | solution.py:236
  32.2 0.0 collective-permute-done.3
  32.2 0.8 %collective-permute-start.8 = (bf16[256,128]{1,0:T(8,128)(2,1)S(1)}, bf16[256,128]{1,0:T(8,128)(2,1)S(1)}, u32[]{:S(2)}, u32[]{:S(2)}) collective-permute-start(bf16[256,128]{1,0:T(8,128)(2,1)S(1)} %get-tuple-element.19), channel_id=1, source_target_pairs={{0,2},{1,3},{2,0},{3,1},{4,6},{5,7},{6,4},{7,5},{8,10},{9,11},{10,... | collective-permute-start | bytes 196616 | tf_op jit(solution)/shard_map/ppermute | solution.py:236
  33.0 0.9 %collective-permute-done.4 = bf16[256,128]{1,0:T(8,128)(2,1)S(1)} collective-permute-done((bf16[256,128]{1,0:T(8,128)(2,1)S(1)}, bf16[256,128]{1,0:T(8,128)(2,1)S(1)}, u32[]{:S(2)}, u32[]{:S(2)}) %collective-permute-start.4) | collective-permute-done | bytes 65568 | tf_op jit(solution)/shard_map/ppermute | solution.py:236
  33.9 0.5 %collective-permute-start.9 = (bf16[256,128]{1,0:T(8,128)(2,1)S(1)}, bf16[256,128]{1,0:T(8,128)(2,1)S(1)}, u32[]{:S(2)}, u32[]{:S(2)}) collective-permute-start(bf16[256,128]{1,0:T(8,128)(2,1)S(1)} %get-tuple-element.20), channel_id=1, source_target_pairs={{0,1},{1,0},{2,3},{3,2},{4,5},{5,4},{6,7},{7,6},{8,9},{9,8},{10,11... | collective-permute-start | bytes 196616 | tf_op jit(solution)/shard_map/ppermute | solution.py:236
  34.4 2.8 %collective-permute-done.5 = bf16[256,128]{1,0:T(8,128)(2,1)S(1)} collective-permute-done((bf16[256,128]{1,0:T(8,128)(2,1)S(1)}, bf16[256,128]{1,0:T(8,128)(2,1)S(1)}, u32[]{:S(2)}, u32[]{:S(2)}) %collective-permute-start.5) | collective-permute-done | bytes 65568 | tf_op jit(solution)/shard_map/ppermute | solution.py:236
  37.2 1.6 %collective-permute-done.6 = bf16[256,128]{1,0:T(8,128)(2,1)S(1)} collective-permute-done((bf16[256,128]{1,0:T(8,128)(2,1)S(1)}, bf16[256,128]{1,0:T(8,128)(2,1)S(1)}, u32[]{:S(2)}, u32[]{:S(2)}) %collective-permute-start.6) | collective-permute-done | bytes 65568 | tf_op jit(solution)/shard_map/ppermute | solution.py:236
  38.8 0.0 collective-permute-done.7
  38.8 0.1 collective-permute-done.8
  38.9 0.0 collective-permute-done.9
  38.9 0.7 %add_multiply_fusion = f32[256,128]{1,0:T(8,128)} fusion(bf16[256,128]{1,0:T(8,128)(2,1)S(1)} %collective-permute-done.9, bf16[256,128]{1,0:T(8,128)(2,1)S(1)} %collective-permute-done.8, bf16[256,128]{1,0:T(8,128)(2,1)S(1)} %collective-permute-done.7, bf16[256,128]{1,0:T(8,128)(2,1)S(1)} %collective-permute-done.6, ...), kind=kLoop, calls=%fused_computation | loop fusion | flops 491520 | bytes 720896 | tf_op jit(solution)/shard_map/mul | solution.py:242
Async XLA Ops:
  0.0 15.1 %collective-permute-start.1 = (bf16[256,1024]{1,0:T(8,128)(2,1)}, bf16[256,1024]{1,0:T(8,128)(2,1)S(1)}, u32[]{:S(2)}, u32[]{:S(2)}) collective-permute-start(bf16[256,1024]{1,0:T(8,128)(2,1)} %refs_0_.3), channel_id=1, source_target_pairs={{0,16},{8,24},{16,0},{24,8},{1,17},{9,25},{17,1},{25,9},{2,18},{10... | collective-permute-start | bytes 1572872 | tf_op jit(solution)/shard_map/ppermute | solution.py:199
  3.0 12.1 %collective-permute-start = (bf16[256,1024]{1,0:T(8,128)(2,1)}, bf16[256,1024]{1,0:T(8,128)(2,1)S(1)}, u32[]{:S(2)}, u32[]{:S(2)}) collective-permute-start(bf16[256,1024]{1,0:T(8,128)(2,1)} %refs_0_.3), channel_id=1, source_target_pairs={{0,8},{8,0},{16,24},{24,16},{1,9},{9,1},{17,25},{25,17},{2,10},{10... | collective-permute-start | bytes 1572872 | tf_op jit(solution)/shard_map/ppermute | solution.py:199
  15.1 1.9 %collective-permute-start.2 = (bf16[256,1024]{1,0:T(8,128)(2,1)S(1)}, bf16[256,1024]{1,0:T(8,128)(2,1)S(1)}, u32[]{:S(2)}, u32[]{:S(2)}) collective-permute-start(bf16[256,1024]{1,0:T(8,128)(2,1)S(1)} %collective-permute-done.1.refs_2_), channel_id=1, source_target_pairs={{0,8},{8,0},{16,24},{24,16},{1,9},{9,1},{17,25},{25,17},{2,10},{10... | collective-permute-start | bytes 1572872 | tf_op jit(solution)/shard_map/ppermute | solution.py:199
  15.1 1.0 %copy-start = (bf16[256,1024]{1,0:T(8,128)(2,1)S(1)}, bf16[256,1024]{1,0:T(8,128)(2,1)}, u32[]{:S(2)}) copy-start(bf16[256,1024]{1,0:T(8,128)(2,1)} %refs_0_.3) | copy-start | bytes 1572868
  16.2 1.0 %copy-start.1 = (bf16[256,1024]{1,0:T(8,128)(2,1)S(1)}, bf16[256,1024]{1,0:T(8,128)(2,1)}, u32[]{:S(2)}) copy-start(bf16[256,1024]{1,0:T(8,128)(2,1)} %refs_0_.3) | copy-start | bytes 1572868
  22.1 10.1 %collective-permute-start.3 = (bf16[256,128]{1,0:T(8,128)(2,1)S(1)}, bf16[256,128]{1,0:T(8,128)(2,1)S(1)}, u32[]{:S(2)}, u32[]{:S(2)}) collective-permute-start(bf16[256,128]{1,0:T(8,128)(2,1)S(1)} %get-tuple-element.14), channel_id=1, source_target_pairs={{0,7},{1,6},{2,5},{3,4},{4,3},{5,2},{6,1},{7,0},{8,15},{9,14},{10,... | collective-permute-start | bytes 196616 | tf_op jit(solution)/shard_map/ppermute | solution.py:236
  26.9 6.9 %collective-permute-start.4 = (bf16[256,128]{1,0:T(8,128)(2,1)S(1)}, bf16[256,128]{1,0:T(8,128)(2,1)S(1)}, u32[]{:S(2)}, u32[]{:S(2)}) collective-permute-start(bf16[256,128]{1,0:T(8,128)(2,1)S(1)} %get-tuple-element.15), channel_id=1, source_target_pairs={{0,6},{1,7},{2,4},{3,5},{4,2},{5,3},{6,0},{7,1},{8,14},{9,15},{10,... | collective-permute-start | bytes 196616 | tf_op jit(solution)/shard_map/ppermute | solution.py:236
  27.2 10.0 %collective-permute-start.5 = (bf16[256,128]{1,0:T(8,128)(2,1)S(1)}, bf16[256,128]{1,0:T(8,128)(2,1)S(1)}, u32[]{:S(2)}, u32[]{:S(2)}) collective-permute-start(bf16[256,128]{1,0:T(8,128)(2,1)S(1)} %get-tuple-element.16), channel_id=1, source_target_pairs={{0,5},{1,4},{2,7},{3,6},{4,1},{5,0},{6,3},{7,2},{8,13},{9,12},{10,... | collective-permute-start | bytes 196616 | tf_op jit(solution)/shard_map/ppermute | solution.py:236
  27.9 10.9 %collective-permute-start.6 = (bf16[256,128]{1,0:T(8,128)(2,1)S(1)}, bf16[256,128]{1,0:T(8,128)(2,1)S(1)}, u32[]{:S(2)}, u32[]{:S(2)}) collective-permute-start(bf16[256,128]{1,0:T(8,128)(2,1)S(1)} %get-tuple-element.17), channel_id=1, source_target_pairs={{0,4},{1,5},{2,6},{3,7},{4,0},{5,1},{6,2},{7,3},{8,12},{9,13},{10,... | collective-permute-start | bytes 196616 | tf_op jit(solution)/shard_map/ppermute | solution.py:236
  30.0 8.8 %collective-permute-start.7 = (bf16[256,128]{1,0:T(8,128)(2,1)S(1)}, bf16[256,128]{1,0:T(8,128)(2,1)S(1)}, u32[]{:S(2)}, u32[]{:S(2)}) collective-permute-start(bf16[256,128]{1,0:T(8,128)(2,1)S(1)} %get-tuple-element.18), channel_id=1, source_target_pairs={{0,3},{1,2},{2,1},{3,0},{4,7},{5,6},{6,5},{7,4},{8,11},{9,10},{10,... | collective-permute-start | bytes 196616 | tf_op jit(solution)/shard_map/ppermute | solution.py:236
  32.2 6.7 %collective-permute-start.8 = (bf16[256,128]{1,0:T(8,128)(2,1)S(1)}, bf16[256,128]{1,0:T(8,128)(2,1)S(1)}, u32[]{:S(2)}, u32[]{:S(2)}) collective-permute-start(bf16[256,128]{1,0:T(8,128)(2,1)S(1)} %get-tuple-element.19), channel_id=1, source_target_pairs={{0,2},{1,3},{2,0},{3,1},{4,6},{5,7},{6,4},{7,5},{8,10},{9,11},{10,... | collective-permute-start | bytes 196616 | tf_op jit(solution)/shard_map/ppermute | solution.py:236
  33.9 5.0 %collective-permute-start.9 = (bf16[256,128]{1,0:T(8,128)(2,1)S(1)}, bf16[256,128]{1,0:T(8,128)(2,1)S(1)}, u32[]{:S(2)}, u32[]{:S(2)}) collective-permute-start(bf16[256,128]{1,0:T(8,128)(2,1)S(1)} %get-tuple-element.20), channel_id=1, source_target_pairs={{0,1},{1,0},{2,3},{3,2},{4,5},{5,4},{6,7},{7,6},{8,9},{9,8},{10,11... | collective-permute-start | bytes 196616 | tf_op jit(solution)/shard_map/ppermute | solution.py:236
where the time goes:
time: 39.9 us; the launch traced here: 39.7 us
  waiting for transfers between devices  17.9 us (45%)
  starting transfers between devices  14.4 us (36%)
  Pallas kernels  5.4 us (14%)
  local copies, waits for them, and re-layouts  1.22 us (3%)
  other arithmetic  0.73 us (2%)
    ppermute x3, waiting for transfers between devices, swap(): return lax.ppermute(x, 'row', [(i, i ^ bit) for i in range(slots)])  12.5 us
    ppermute x7, starting transfers between devices, per_device(): lax.ppermute(outs[p], 'col', [(i, i ^ p) for i in range(peers)])  11.4 us
    ppermute x7, waiting for transfers between devices, per_device(): lax.ppermute(outs[p], 'col', [(i, i ^ p) for i in range(peers)])  5.37 us
    pallas_call x1, Pallas kernels, per_device(): pl.pallas_call(functools.partial(body, slots=slots, peers=peers, total=to...  4.91 us
    ppermute x3, starting transfers between devices, swap(): return lax.ppermute(x, 'row', [(i, i ^ bit) for i in range(slots)])  3 us
    unnamed x4, local copies, waits for them, and re-layouts  1.22 us
  transfers between devices with their start and end apart: 10, of which 6 were waited for; matrix products, arithmetic and copies ran while one was open for 0% of the time, Pallas kernels for 1%

commit v1 on v0

--- a/solution.py
+++ b/solution.py
@@ -122,12 +122,13 @@
     fisher_sums(grads, store)
 
 
-def body(sums_ref, *refs, slots, peers, total):
+def body(sums_ref, *refs, slots, total, kept, lent):
     grads = refs[:slots]
-    outs = refs[slots : slots + peers]
-    packed, rows, inverse, white = refs[slots + peers :]
+    outs = refs[slots : slots + len(kept)]
+    *lent_refs, packed, rows, inverse, white = refs[slots + len(kept) :]
     count, width = grads[0].shape
-    block = outs[0].shape[1]
+    block = lent_refs[0].shape[1]
+    peers = len(kept) + sum(len(part) for part in lent)
     groups = width // LANES
 
     lane = lax.broadcasted_iota(jnp.int32, (BW, LANES), 1)
@@ -180,9 +181,15 @@
             stacked.append(white_rows(pl.multiple_of(start, block), block))
         out = times_transposed(mine, jnp.concatenate(stacked, axis=0))
         for i in range(2):
-            outs[first + i][...] = out[:, i * block : (i + 1) * block].astype(
-                outs[first + i].dtype
-            )
+            p = first + i
+            part = out[:, i * block : (i + 1) * block]
+            if p in kept:
+                ref = outs[kept.index(p)]
+                ref[...] = part.astype(ref.dtype)
+            for ref, ps in zip(lent_refs, lent):
+                if p in ps:
+                    at = ps.index(p) * count
+                    ref[at : at + count, :] = part.astype(ref.dtype)
 
 
 def per_device(grads):
@@ -192,6 +199,10 @@
     total = count * slots
     block = total // peers
     groups = width // LANES
+    straight = list(range(peers // 2, peers * 3 // 4))
+    joint = [p for p in reversed(range(2, peers, 2)) if p not in straight]
+    kept = [0] + joint + straight
+    lent = [[p + 1 for p in joint], [1]]
     vmem = pl.BlockSpec(memory_space=pltpu.VMEM)
     params = pltpu.CompilerParams(vmem_limit_bytes=VMEM_LIMIT)
 
@@ -215,14 +226,15 @@
         compiler_params=params,
     )(*near)
 
-    outs = pl.pallas_call(
-        functools.partial(body, slots=slots, peers=peers, total=total),
+    *outs, urgent, loan = pl.pallas_call(
+        functools.partial(body, slots=slots, total=total, kept=kept, lent=lent),
         in_specs=[vmem] * (slots + 1),
-        out_specs=[vmem] * peers,
+        out_specs=[vmem] * (len(kept) + 2),
         out_shape=[
-            jax.ShapeDtypeStruct((count, block), jnp.bfloat16 if p else jnp.float32)
-            for p in range(peers)
-        ],
+            jax.ShapeDtypeStruct((count, block), jnp.bfloat16 if p in straight else jnp.float32)
+            for p in kept
+        ]
+        + [jax.ShapeDtypeStruct((count * len(part), block), jnp.bfloat16) for part in lent],
         scratch_shapes=[
             pltpu.VMEM((groups * BW, LANES), jnp.float32),
             pltpu.VMEM((BW * SUB, LANES), jnp.float32),
@@ -231,12 +243,22 @@
         ],
         compiler_params=params,
     )(sums, *[held[t] for t in range(slots)])
-
-    got = [
-        lax.ppermute(outs[p], "col", [(i, i ^ p) for i in range(peers)])
-        for p in reversed(range(1, peers))
+    own = dict(zip(kept, outs))
+
+    def exchange(x, p):
+        return lax.ppermute(x, "col", [(i, i ^ p) for i in range(peers)])
+
+    urgent = exchange(urgent, 1)
+    got = [exchange(own[p], p) for p in reversed(straight)]
+    loan = exchange(loan, 1)
+    borrowed = [
+        array[i * count : (i + 1) * count].astype(jnp.float32)
+        for array, part in zip((urgent, loan), lent)
+        for i in range(len(part))
     ]
-    kernel = outs[0]
+    for p, more in zip(joint, borrowed):
+        got.append(exchange((own[p] + more).astype(jnp.bfloat16), p))
+    kernel = own[0] + borrowed[-1]
     for part in got:
         kernel = kernel + part.astype(jnp.float32)
     return kernel * (width * peers) ** (-0.5)

time: 39.9 us -> 38 us (0.952)
  starting transfers between devices: 14.4 us -> 13 us
  waiting for transfers between devices: 17.9 us -> 17.4 us
    ppermute x7 -> x6, starting transfers between devices: 11.4 us -> 10 us  [exchange(): return lax.ppermute(x, 'col', [(i, i ^ p) for i in range(peers)])]
    ppermute x7 -> x6, waiting for transfers between devices: 5.37 us -> 4.9 us  [exchange(): return lax.ppermute(x, 'col', [(i, i ^ p) for i in range(peers)])]
  transfers between devices with their start and end apart: 10 -> 9, of which waited for: 6 -> 5; matrix products, arithmetic and copies ran while one was open for 0% -> 0% of each run, Pallas kernels for 1% -> 1%
where the time goes in v1:
time: 38 us; the launch traced here: 37.8 us
  waiting for transfers between devices  17.4 us (46%)
  starting transfers between devices  13 us (34%)
  Pallas kernels  5.4 us (14%)
  local copies, waits for them, and re-layouts  1.22 us (3%)
  other arithmetic  0.75 us (2%)
    ppermute x3, waiting for transfers between devices, swap(): return lax.ppermute(x, 'row', [(i, i ^ bit) for i in range(slots)])  12.5 us
    ppermute x6, starting transfers between devices, exchange(): return lax.ppermute(x, 'col', [(i, i ^ p) for i in range(peers)])  10 us
    pallas_call x1, Pallas kernels, per_device(): pl.pallas_call(functools.partial(body, slots=slots, total=total, kept=kep...  4.91 us
    ppermute x6, waiting for transfers between devices, exchange(): return lax.ppermute(x, 'col', [(i, i ^ p) for i in range(peers)])  4.9 us
    ppermute x3, starting transfers between devices, swap(): return lax.ppermute(x, 'row', [(i, i ^ bit) for i in range(slots)])  3 us
    unnamed x4, local copies, waits for them, and re-layouts  1.22 us
  transfers between devices with their start and end apart: 9, of which 5 were waited for; matrix products, arithmetic and copies ran while one was open for 0% of the time, Pallas kernels for 1%

profile of v1, /device:TPU:0, one launch (start us, length us, event | category | flops | bytes accessed | tf_op | source)
XLA Modules:
  0.0 37.8 jit_solution(2273162836792376956)
XLA Ops:
  0.0 3.0 %collective-permute-start.1 = (bf16[256,1024]{1,0:T(8,128)(2,1)}, bf16[256,1024]{1,0:T(8,128)(2,1)S(1)}, u32[]{:S(2)}, u32[]{:S(2)}) collective-permute-start(bf16[256,1024]{1,0:T(8,128)(2,1)} %refs_0_.3), channel_id=1, source_target_pairs={{0,16},{8,24},{16,0},{24,8},{1,17},{9,25},{17,1},{25,9},{2,18},{10... | collective-permute-start | bytes 1572872 | tf_op jit(solution)/shard_map/ppermute | solution.py:210
  3.0 0.0 collective-permute-start
  3.0 12.1 %collective-permute-done.1.refs_2_ = bf16[256,1024]{1,0:T(8,128)(2,1)S(1)} collective-permute-done((bf16[256,1024]{1,0:T(8,128)(2,1)}, bf16[256,1024]{1,0:T(8,128)(2,1)S(1)}, u32[]{:S(2)}, u32[]{:S(2)}) %collective-permute-start.1) | collective-permute-done | bytes 524320 | tf_op jit(solution)/shard_map/ppermute | solution.py:210
  15.1 0.0 collective-permute-start.2
  15.1 0.0 collective-permute-done.refs_1_
  15.1 0.0 copy-start
  15.1 1.0 %copy-done = bf16[256,1024]{1,0:T(8,128)(2,1)S(1)} copy-done((bf16[256,1024]{1,0:T(8,128)(2,1)S(1)}, bf16[256,1024]{1,0:T(8,128)(2,1)}, u32[]{:S(2)}) %copy-start) | copy-done | bytes 524312
  16.2 0.0 copy-start.1
  16.2 0.5 %shard_map.17.sums_ref = f32[8,64,128]{2,1,0:T(8,128)S(1)} custom-call(bf16[256,1024]{1,0:T(8,128)(2,1)S(1)} %copy-done, bf16[256,1024]{1,0:T(8,128)(2,1)S(1)} %collective-permute-done.refs_1_), custom_call_target="tpu_custom_call" | custom-call | tf_op jit(solution)/shard_map/pallas_call | solution.py:221
  16.7 0.4 collective-permute-done.2.refs_3_
  17.0 0.2 copy-done.1
  17.2 4.9 %shard_map.18 = (f32[256,128]{1,0:T(8,128)S(1)}, f32[256,128]{1,0:T(8,128)S(1)}, f32[256,128]{1,0:T(8,128)S(1)}, bf16[256,128]{1,0:T(8,128)(2,1)S(1)}, bf16[256,...) custom-call(f32[8,64,128]{2,1,0:T(8,128)S(1)} %shard_map.17.sums_ref, ...), custom_call_target="tpu_custom_call" | custom-call | tf_op jit(solution)/shard_map/pallas_call | solution.py:229
  22.1 1.8 %collective-permute-start.6 = (bf16[512,128]{1,0:T(8,128)(2,1)S(1)}, bf16[512,128]{1,0:T(8,128)(2,1)S(1)}, u32[]{:S(2)}, u32[]{:S(2)}) collective-permute-start(bf16[512,128]{1,0:T(8,128)(2,1)S(1)} %get-tuple-element.17), channel_id=1, source_target_pairs={{0,1},{1,0},{2,3},{3,2},{4,5},{5,4},{6,7},{7,6},{8,9},{9,8},{10,11... | collective-permute-start | bytes 393224 | tf_op jit(solution)/shard_map/ppermute | solution.py:249
  23.9 0.3 collective-permute-start.3
  24.2 3.7 %collective-permute-start.4 = (bf16[256,128]{1,0:T(8,128)(2,1)S(1)}, bf16[256,128]{1,0:T(8,128)(2,1)S(1)}, u32[]{:S(2)}, u32[]{:S(2)}) collective-permute-start(bf16[256,128]{1,0:T(8,128)(2,1)S(1)} %get-tuple-element.14), channel_id=1, source_target_pairs={{0,5},{1,4},{2,7},{3,6},{4,1},{5,0},{6,3},{7,2},{8,13},{9,12},{10,... | collective-permute-start | bytes 196616 | tf_op jit(solution)/shard_map/ppermute | solution.py:249
  28.0 0.3 collective-permute-start.5
  28.3 0.3 collective-permute-done.6
  28.6 3.9 %collective-permute-start.7 = (bf16[256,128]{1,0:T(8,128)(2,1)S(1)}, bf16[256,128]{1,0:T(8,128)(2,1)S(1)}, u32[]{:S(2)}, u32[]{:S(2)}) collective-permute-start(bf16[256,128]{1,0:T(8,128)(2,1)S(1)} %get-tuple-element.19), channel_id=1, source_target_pairs={{0,6},{1,7},{2,4},{3,5},{4,2},{5,3},{6,0},{7,1},{8,14},{9,15},{10,... | collective-permute-start | bytes 196616 | tf_op jit(solution)/shard_map/ppermute | solution.py:249
  32.5 0.0 collective-permute-start.8
  32.5 0.0 collective-permute-done.3
  32.5 0.0 collective-permute-done.4
  32.5 4.0 %collective-permute-done.5 = bf16[256,128]{1,0:T(8,128)(2,1)S(1)} collective-permute-done((bf16[256,128]{1,0:T(8,128)(2,1)S(1)}, bf16[256,128]{1,0:T(8,128)(2,1)S(1)}, u32[]{:S(2)}, u32[]{:S(2)}) %collective-permute-start.5) | collective-permute-done | bytes 65568 | tf_op jit(solution)/shard_map/ppermute | solution.py:249
  36.5 0.0 collective-permute-done.7
  36.5 0.6 %collective-permute-done.8 = bf16[256,128]{1,0:T(8,128)(2,1)S(1)} collective-permute-done((bf16[256,128]{1,0:T(8,128)(2,1)S(1)}, bf16[256,128]{1,0:T(8,128)(2,1)S(1)}, u32[]{:S(2)}, u32[]{:S(2)}) %collective-permute-start.8) | collective-permute-done | bytes 65568 | tf_op jit(solution)/shard_map/ppermute | solution.py:249
  37.1 0.7 %add_multiply_fusion = f32[256,128]{1,0:T(8,128)} fusion(bf16[256,128]{1,0:T(8,128)(2,1)S(1)} %collective-permute-done.8, bf16[256,128]{1,0:T(8,128)(2,1)S(1)} %collective-permute-done.7, bf16[256,128]{1,0:T(8,128)(2,1)S(1)} %collective-permute-done.5, bf16[256,128]{1,0:T(8,128)(2,1)S(1)} %collective-permute-done.4, f32[256,128]{1,0:T(8,128)S(1)} %get-tuple-element.12, ...), kind=kLoop, calls=%fused_computation | loop fusion | flops 360448 | bytes 589824 | tf_op jit(solution)/shard_map/mul | solution.py:264
  (1 shorter events, 0.0 us)
Async XLA Ops:
  0.0 15.1 %collective-permute-start.1 = (bf16[256,1024]{1,0:T(8,128)(2,1)}, bf16[256,1024]{1,0:T(8,128)(2,1)S(1)}, u32[]{:S(2)}, u32[]{:S(2)}) collective-permute-start(bf16[256,1024]{1,0:T(8,128)(2,1)} %refs_0_.3), channel_id=1, source_target_pairs={{0,16},{8,24},{16,0},{24,8},{1,17},{9,25},{17,1},{25,9},{2,18},{10... | collective-permute-start | bytes 1572872 | tf_op jit(solution)/shard_map/ppermute | solution.py:210
  3.0 12.1 %collective-permute-start = (bf16[256,1024]{1,0:T(8,128)(2,1)}, bf16[256,1024]{1,0:T(8,128)(2,1)S(1)}, u32[]{:S(2)}, u32[]{:S(2)}) collective-permute-start(bf16[256,1024]{1,0:T(8,128)(2,1)} %refs_0_.3), channel_id=1, source_target_pairs={{0,8},{8,0},{16,24},{24,16},{1,9},{9,1},{17,25},{25,17},{2,10},{10... | collective-permute-start | bytes 1572872 | tf_op jit(solution)/shard_map/ppermute | solution.py:210
  15.1 1.9 %collective-permute-start.2 = (bf16[256,1024]{1,0:T(8,128)(2,1)S(1)}, bf16[256,1024]{1,0:T(8,128)(2,1)S(1)}, u32[]{:S(2)}, u32[]{:S(2)}) collective-permute-start(bf16[256,1024]{1,0:T(8,128)(2,1)S(1)} %collective-permute-done.1.refs_2_), channel_id=1, source_target_pairs={{0,8},{8,0},{16,24},{24,16},{1,9},{9,1},{17,25},{25,17},{2,10},{10... | collective-permute-start | bytes 1572872 | tf_op jit(solution)/shard_map/ppermute | solution.py:210
  15.1 1.0 %copy-start = (bf16[256,1024]{1,0:T(8,128)(2,1)S(1)}, bf16[256,1024]{1,0:T(8,128)(2,1)}, u32[]{:S(2)}) copy-start(bf16[256,1024]{1,0:T(8,128)(2,1)} %refs_0_.3) | copy-start | bytes 1572868
  16.2 1.0 %copy-start.1 = (bf16[256,1024]{1,0:T(8,128)(2,1)S(1)}, bf16[256,1024]{1,0:T(8,128)(2,1)}, u32[]{:S(2)}) copy-start(bf16[256,1024]{1,0:T(8,128)(2,1)} %refs_0_.3) | copy-start | bytes 1572868
  22.1 6.4 %collective-permute-start.6 = (bf16[512,128]{1,0:T(8,128)(2,1)S(1)}, bf16[512,128]{1,0:T(8,128)(2,1)S(1)}, u32[]{:S(2)}, u32[]{:S(2)}) collective-permute-start(bf16[512,128]{1,0:T(8,128)(2,1)S(1)} %get-tuple-element.17), channel_id=1, source_target_pairs={{0,1},{1,0},{2,3},{3,2},{4,5},{5,4},{6,7},{7,6},{8,9},{9,8},{10,11... | collective-permute-start | bytes 393224 | tf_op jit(solution)/shard_map/ppermute | solution.py:249
  23.9 8.6 %collective-permute-start.3 = (bf16[256,128]{1,0:T(8,128)(2,1)S(1)}, bf16[256,128]{1,0:T(8,128)(2,1)S(1)}, u32[]{:S(2)}, u32[]{:S(2)}) collective-permute-start(bf16[256,128]{1,0:T(8,128)(2,1)S(1)} %get-tuple-element.13), channel_id=1, source_target_pairs={{0,1},{1,0},{2,3},{3,2},{4,5},{5,4},{6,7},{7,6},{8,9},{9,8},{10,11... | collective-permute-start | bytes 196616 | tf_op jit(solution)/shard_map/ppermute | solution.py:249
  24.2 8.3 %collective-permute-start.4 = (bf16[256,128]{1,0:T(8,128)(2,1)S(1)}, bf16[256,128]{1,0:T(8,128)(2,1)S(1)}, u32[]{:S(2)}, u32[]{:S(2)}) collective-permute-start(bf16[256,128]{1,0:T(8,128)(2,1)S(1)} %get-tuple-element.14), channel_id=1, source_target_pairs={{0,5},{1,4},{2,7},{3,6},{4,1},{5,0},{6,3},{7,2},{8,13},{9,12},{10,... | collective-permute-start | bytes 196616 | tf_op jit(solution)/shard_map/ppermute | solution.py:249
  28.0 8.5 %collective-permute-start.5 = (bf16[256,128]{1,0:T(8,128)(2,1)S(1)}, bf16[256,128]{1,0:T(8,128)(2,1)S(1)}, u32[]{:S(2)}, u32[]{:S(2)}) collective-permute-start(bf16[256,128]{1,0:T(8,128)(2,1)S(1)} %get-tuple-element.15), channel_id=1, source_target_pairs={{0,4},{1,5},{2,6},{3,7},{4,0},{5,1},{6,2},{7,3},{8,12},{9,13},{10,... | collective-permute-start | bytes 196616 | tf_op jit(solution)/shard_map/ppermute | solution.py:249
  28.6 7.9 %collective-permute-start.7 = (bf16[256,128]{1,0:T(8,128)(2,1)S(1)}, bf16[256,128]{1,0:T(8,128)(2,1)S(1)}, u32[]{:S(2)}, u32[]{:S(2)}) collective-permute-start(bf16[256,128]{1,0:T(8,128)(2,1)S(1)} %get-tuple-element.19), channel_id=1, source_target_pairs={{0,6},{1,7},{2,4},{3,5},{4,2},{5,3},{6,0},{7,1},{8,14},{9,15},{10,... | collective-permute-start | bytes 196616 | tf_op jit(solution)/shard_map/ppermute | solution.py:249
  32.5 4.6 %collective-permute-start.8 = (bf16[256,128]{1,0:T(8,128)(2,1)S(1)}, bf16[256,128]{1,0:T(8,128)(2,1)S(1)}, u32[]{:S(2)}, u32[]{:S(2)}) collective-permute-start(bf16[256,128]{1,0:T(8,128)(2,1)S(1)} %get-tuple-element.20), channel_id=1, source_target_pairs={{0,2},{1,3},{2,0},{3,1},{4,6},{5,7},{6,4},{7,5},{8,10},{9,11},{10,... | collective-permute-start | bytes 196616 | tf_op jit(solution)/shard_map/ppermute | solution.py:249

commit v2 on v0

v2 whole, which is shorter than its diff:
```python
import functools

import jax
import jax.numpy as jnp
from jax import lax
from jax.experimental import pallas as pl
from jax.experimental.pallas import tpu as pltpu
from jax.sharding import PartitionSpec as P

BW = 64
LANES = 128
SUB = 8
VMEM_LIMIT = 16 << 20


def lane_gather(rows, index):
    return jnp.take_along_axis(rows, index, axis=1, mode="promise_in_bounds")


def gram(x):
    return lax.dot_general(x, x, (((0,), (0,)), ((), ())), preferred_element_type=jnp.float32)


def times(x, y):
    return lax.dot_general(x, y, (((1,), (0,)), ((), ())), preferred_element_type=jnp.float32)


def times_transposed(x, y):
    return lax.dot_general(x, y, (((1,), (1,)), ((), ())), preferred_element_type=jnp.float32)


def fisher_sums(grads, store):
    width = grads[0].shape[1]
    wide = min(2 * LANES, width)
    low = lax.broadcasted_iota(jnp.int32, (BW, LANES), 1) < BW
    for w in range(width // wide):
        x = jnp.concatenate([g[:, w * wide : (w + 1) * wide] for g in grads], axis=0)
        square = gram(x)
        for h in range(wide // LANES):
            at = h * LANES
            tile = square[at : at + LANES, at : at + LANES]
            store(w * (wide // LANES) + h, jnp.where(low, tile[:BW], tile[BW:]))


def broadcast_row(block, i):
    return jnp.broadcast_to(block[i : i + 1, :], block.shape)


def to_lanes(packed, rows, groups):
    lane = lax.broadcasted_iota(jnp.int32, (BW, LANES), 1)
    even = (lane // SUB) % 2 == 0
    for lo in range(SUB):
        parts = []
        for s in range(SUB):
            part = packed[pl.ds((s % groups) * BW + lo, SUB, stride=SUB), :]
            parts += [part, part]
        turned = jnp.concatenate(parts, axis=0).T
        rows[pl.ds(lo, BW, stride=SUB), :] = jnp.where(even, turned[:BW], turned[BW:])


def from_lanes(rows, inverse, groups):
    low = lax.broadcasted_iota(jnp.int32, (SUB, LANES), 1) < BW
    for lo in range(SUB):
        half = rows[pl.ds(lo, BW, stride=SUB), :]
        turned = jnp.concatenate([half, half], axis=0).T
        for s in range(groups):
            for h in range(2):
                at = (s * 2 + h) * SUB
                tile = turned[at : at + SUB]
                tile = jnp.where(low, 0.0, tile) if h else jnp.where(low, tile, 0.0)
                inverse[pl.ds((s * 2 + h) * BW + lo, SUB, stride=SUB), :] = tile


def factor(rows):
    lane = lax.broadcasted_iota(jnp.int32, (SUB, LANES), 1)
    sub = lax.broadcasted_iota(jnp.int32, (SUB, LANES), 0)
    chunk = lane % SUB
    column = chunk * SUB + sub
    base = lane - chunk

    def at(k):
        return slice(k * SUB, (k + 1) * SUB)

    for p in range(BW // SUB):
        first = p * SUB
        panel = [rows[at(first + q), :] for q in range(SUB)]
        near = [lane_gather(row, base + p) for row in panel]
        inside = chunk == p
        steps = []
        for q in range(SUB):
            here = column == first + q
            pivot = broadcast_row(near[q], q)
            inv = 1.0 / pivot
            step = jnp.where(here, 1.0, panel[q]) * inv
            near_step = near[q] * inv
            for k in range(q + 1, SUB):
                down = broadcast_row(near[q], k)
                panel[k] = jnp.where(here, 0.0, panel[k]) - down * step
                near[k] = near[k] - down * near_step
            steps.append(jnp.where(jnp.logical_and(inside, sub > q), 0.0, step))
            rows[at(first + q), :] = jnp.where(
                column < first + q, panel[q], jnp.where(here, 1.0, 0.0)
            ) * lax.rsqrt(pivot)
        for hi in range(p + 1, BW // SUB):
            downs = [lane_gather(row, base + hi) for row in panel]
            for lo in range(SUB):
                k = hi * SUB + lo
                row = jnp.where(inside, 0.0, rows[at(k), :])
                for q in range(SUB):
                    row = row - broadcast_row(downs[q], lo) * steps[q]
                rows[at(k), :] = row


def sums_body(*refs, resumed):
    *grads, sums = refs
    before = grads.pop(0) if resumed else None

    def store(s, value):
        sums[s] = before[s] + value if resumed else value

    fisher_sums(grads, store)


def body(sums_ref, *refs, slots, total, first):
    grads = refs[:slots]
    *refs_out, white, packed, rows, inverse = refs[slots:]
    count, width = grads[0].shape
    groups = width // LANES

    lane = lax.broadcasted_iota(jnp.int32, (BW, LANES), 1)
    sub = lax.broadcasted_iota(jnp.int32, (BW, LANES), 0)
    unit = jnp.where(sub == lane % BW, 0.1, 0.0)

    def store(s, value):
        packed[s * BW : (s + 1) * BW, :] = (sums_ref[s] + value) * (1.0 / total) + unit

    fisher_sums(grads[slots // 2 + 1 :: 2], store)
    to_lanes(packed, rows, groups)
    factor(rows)
    from_lanes(rows, inverse, groups)

    wide = min(2 * LANES, width)
    pairs = wide // LANES
    zero = jnp.zeros((LANES, LANES), jnp.float32)
    for w in range(width // wide):
        blocks = []
        for h in range(pairs):
            s = w * pairs + h
            tile = inverse[s * LANES : (s + 1) * LANES, :]
            blocks.append(jnp.concatenate([tile if i == h else zero for i in range(pairs)], axis=1))
        matrix = jnp.concatenate(blocks, axis=0)
        high = matrix.astype(jnp.bfloat16)
        rest = (matrix - high.astype(jnp.float32)).astype(jnp.bfloat16)
        x = jnp.concatenate([g[:, w * wide : (w + 1) * wide] for g in grads], axis=0)
        out = (times(x, high) + times(x, rest)).astype(jnp.bfloat16)
        for h in range(pairs):
            white[w * pairs + h] = out[:, h * LANES : (h + 1) * LANES]

    products(white, refs_out, first, count)


def products(white, outs, asked, count):
    groups = white.shape[0]
    block = outs[0].shape[1]
    row = lax.axis_index("row")
    col = lax.axis_index("col")
    per_slot = count // block

    def white_rows(start, size):
        return jnp.concatenate([white[s, pl.ds(start, size), :] for s in range(groups)], axis=1)

    mine = white_rows(0, count)
    places = [(ref, i * count, p) for ref, ps in zip(outs, asked) for i, p in enumerate(ps)]
    for first in range(0, len(places), 2):
        pair = places[first : first + 2]
        stacked = []
        for _, _, p in pair:
            peer = col ^ p
            start = ((peer // per_slot) ^ row) * count + (peer % per_slot) * block
            stacked.append(white_rows(pl.multiple_of(start, block), block))
        out = times_transposed(mine, jnp.concatenate(stacked, axis=0))
        for i, (ref, at, _) in enumerate(pair):
            part = out[:, i * block : (i + 1) * block]
            ref[at : at + count, :] = part.astype(ref.dtype)


def rest_body(white, *outs, asked, count):
    products(white, outs, asked, count)


def per_device(grads):
    slots = lax.axis_size("row")
    peers = lax.axis_size("col")
    count, width = grads.shape
    total = count * slots
    block = total // peers
    groups = width // LANES
    straight = list(range(peers // 2, peers * 3 // 4))
    joint = [p for p in reversed(range(2, peers, 2)) if p not in straight]
    first = [[p + 1 for p in joint]] + [[p] for p in straight]
    second = [[p] for p in joint] + [[0], [1]]
    vmem = pl.BlockSpec(memory_space=pltpu.VMEM)
    params = pltpu.CompilerParams(vmem_limit_bytes=VMEM_LIMIT)

    def swap(x, bit):
        return lax.ppermute(x, "row", [(i, i ^ bit) for i in range(slots)])

    def sums_of(arrays, resumed):
        return pl.pallas_call(
            functools.partial(sums_body, resumed=resumed),
            in_specs=[vmem] * len(arrays),
            out_specs=vmem,
            out_shape=jax.ShapeDtypeStruct((groups, BW, LANES), jnp.float32),
            compiler_params=params,
        )(*arrays)

    far = slots // 2
    held = {0: grads, far: swap(grads, far)}
    bit = far // 2
    while bit:
        for t in list(held):
            held[t ^ bit] = swap(held[t], bit)
        bit //= 2

    sums = sums_of([held[t] for t in range(far)], False)
    sums = sums_of([sums] + [held[t] for t in range(far, slots, 2)], True)

    def results(asked, dtypes):
        return [
            jax.ShapeDtypeStruct((count * len(ps), block), dtype)
            for ps, dtype in zip(asked, dtypes)
        ]

    urgent, *sent, white = pl.pallas_call(
        functools.partial(body, slots=slots, total=total, first=first),
        in_specs=[vmem] * (slots + 1),
        out_specs=[vmem] * (len(first) + 1),
        out_shape=results(first, [jnp.bfloat16] * len(first))
        + [jax.ShapeDtypeStruct((groups, total, LANES), jnp.bfloat16)],
        scratch_shapes=[
            pltpu.VMEM((groups * BW, LANES), jnp.float32),
            pltpu.VMEM((BW * SUB, LANES), jnp.float32),
            pltpu.VMEM((groups * LANES, LANES), jnp.float32),
        ],
        compiler_params=params,
    )(sums, *[held[t] for t in range(slots)])
    *kept, own, loan = pl.pallas_call(
        functools.partial(rest_body, asked=second, count=count),
        in_specs=[vmem],
        out_specs=[vmem] * len(second),
        out_shape=results(second, [jnp.float32] * (len(second) - 1) + [jnp.bfloat16]),
        compiler_params=params,
    )(white)

    def exchange(x, p):
        return lax.ppermute(x, "col", [(i, i ^ p) for i in range(peers)])

    urgent = exchange(urgent, 1)
    got = [exchange(x, p) for p, x in reversed(list(zip(straight, sent)))]
    loan = exchange(loan, 1)
    for i, p in enumerate(joint):
        both = kept[i] + urgent[i * count : (i + 1) * count].astype(jnp.float32)
        got.append(exchange(both.astype(jnp.bfloat16), p))
    kernel = own
    for part in got[: len(straight)]:
        kernel = kernel + part.astype(jnp.float32)
    kernel = lax.optimization_barrier(kernel)
    for part in [*got[len(straight) :], loan]:
        kernel = kernel + part.astype(jnp.float32)
    return kernel * (width * peers) ** (-0.5)


def solution(mesh):
    return jax.shard_map(
        per_device,
        mesh=mesh,
        in_specs=(P("row", "col"),),
        out_specs=P("row", "col"),
        check_vma=False,
    )
```

time: 39.9 us -> 37.8 us (0.947)
  starting transfers between devices: 14.4 us -> 12.9 us
  waiting for transfers between devices: 17.9 us -> 17.1 us
    ppermute x7 -> x6, starting transfers between devices: 11.4 us -> 9.9 us  [exchange(): return lax.ppermute(x, 'col', [(i, i ^ p) for i in range(peers)])]
    ppermute x7 -> x6, waiting for transfers between devices: 5.37 us -> 4.92 us  [exchange(): return lax.ppermute(x, 'col', [(i, i ^ p) for i in range(peers)])]
    pallas_call x2 -> x4, Pallas kernels: 5.4 us -> 5.58 us  [the longest x1 4.27 us: per_device(): pl.pallas_call(functools.partial(body, slots=slots, total=total, first=fi...]
  transfers between devices with their start and end apart: 10 -> 9, of which waited for: 6 -> 3; matrix products, arithmetic and copies ran while one was open for 0% -> 0% of each run, Pallas kernels for 1% -> 3%
where the time goes in v2:
time: 37.8 us; the launch traced here: 37.6 us
  waiting for transfers between devices  17.1 us (45%)
  starting transfers between devices  12.9 us (34%)
  Pallas kernels  5.58 us (15%)
  local copies, waits for them, and re-layouts  1.21 us (3%)
  other arithmetic  0.74 us (2%)
    ppermute x3, waiting for transfers between devices, swap(): return lax.ppermute(x, 'row', [(i, i ^ bit) for i in range(slots)])  12.1 us
    ppermute x6, starting transfers between devices, exchange(): return lax.ppermute(x, 'col', [(i, i ^ p) for i in range(peers)])  9.9 us
    ppermute x6, waiting for transfers between devices, exchange(): return lax.ppermute(x, 'col', [(i, i ^ p) for i in range(peers)])  4.92 us
    pallas_call x1, Pallas kernels, per_device(): pl.pallas_call(functools.partial(body, slots=slots, total=total, first=fi...  4.27 us
    ppermute x3, starting transfers between devices, swap(): return lax.ppermute(x, 'row', [(i, i ^ bit) for i in range(slots)])  3 us
    unnamed x4, local copies, waits for them, and re-layouts  1.21 us
    pallas_call x2, Pallas kernels, sums_of(): pl.pallas_call(functools.partial(sums_body, resumed=resumed), in_specs=[v...  0.84 us
  transfers between devices with their start and end apart: 9, of which 3 were waited for; matrix products, arithmetic and copies ran while one was open for 0% of the time, Pallas kernels for 3%

profile of v2, /device:TPU:0, one launch (start us, length us, event | category | flops | bytes accessed | tf_op | source)
XLA Modules:
  0.0 37.6 jit_solution(6079894813750706793)
XLA Ops:
  0.0 3.0 %collective-permute-start.1 = (bf16[256,1024]{1,0:T(8,128)(2,1)}, bf16[256,1024]{1,0:T(8,128)(2,1)S(1)}, u32[]{:S(2)}, u32[]{:S(2)}) collective-permute-start(bf16[256,1024]{1,0:T(8,128)(2,1)} %refs_0_.3), channel_id=1, source_target_pairs={{0,16},{8,24},{16,0},{24,8},{1,17},{9,25},{17,1},{25,9},{2,18},{10... | collective-permute-start | bytes 1572872 | tf_op jit(solution)/shard_map/ppermute | solution.py:206
  3.0 0.0 collective-permute-start
  3.0 12.1 %collective-permute-done.1.refs_1_.refs_2_ = bf16[256,1024]{1,0:T(8,128)(2,1)S(1)} collective-permute-done((bf16[256,1024]{1,0:T(8,128)(2,1)}, bf16[256,1024]{1,0:T(8,128)(2,1)S(1)}, u32[]{:S(2)}, u32[]{:S(2)}) %collective-permute-start.1) | collective-permute-done | bytes 524320 | tf_op jit(solution)/shard_map/ppermute | solution.py:206
  15.1 0.0 collective-permute-start.2
  15.1 0.0 collective-permute-done.refs_1_
  15.1 0.0 copy-start
  15.1 1.0 %copy-done = bf16[256,1024]{1,0:T(8,128)(2,1)S(1)} copy-done((bf16[256,1024]{1,0:T(8,128)(2,1)S(1)}, bf16[256,1024]{1,0:T(8,128)(2,1)}, u32[]{:S(2)}) %copy-start) | copy-done | bytes 524312
  16.2 0.0 copy-start.1
  16.2 0.5 %shard_map.17.refs_0_ = f32[8,64,128]{2,1,0:T(8,128)S(1)} custom-call(bf16[256,1024]{1,0:T(8,128)(2,1)S(1)} %copy-done, bf16[256,1024]{1,0:T(8,128)(2,1)S(1)} %collective-permute-done.refs_1_), custom_call_target="tpu_custom_call" | custom-call | tf_op jit(solution)/shard_map/pallas_call | solution.py:209
  16.7 0.4 shard_map.18.sums_ref
  17.0 0.0 collective-permute-done.2.refs_3_
  17.0 0.2 copy-done.1
  17.2 4.3 %shard_map.19 = (bf16[512,128]{1,0:T(8,128)(2,1)S(1)}, bf16[256,128]{1,0:T(8,128)(2,1)S(1)}, bf16[256,128]{1,0:T(8,128)(2,1)S(1)}, bf16[8,1024,128]{2,1,0:T(8,128)(2,1)S(1)}) custom-call(f32[8,64,128]{2,1,0:T(8,128)S(1)} %shard_map.18.sums_ref, bf16[256,1024]{1,0:T(8,128)(2,1)S(1)} %copy-done.1, bf16[256,1024]{1,0:T(8,128)(2,1)S(1)} %collective-permute-done.refs_1_, ...), custom_call_target="tpu_custom_call" | custom-call | tf_op jit(solution)/shard_map/pallas_call | solution.py:234
  21.5 1.8 %collective-permute-start.5 = (bf16[512,128]{1,0:T(8,128)(2,1)S(1)}, bf16[512,128]{1,0:T(8,128)(2,1)S(1)}, u32[]{:S(2)}, u32[]{:S(2)}) collective-permute-start(bf16[512,128]{1,0:T(8,128)(2,1)S(1)} %get-tuple-element.18), channel_id=1, source_target_pairs={{0,1},{1,0},{2,3},{3,2},{4,5},{5,4},{6,7},{7,6},{8,9},{9,8},{10,11... | collective-permute-start | bytes 393224 | tf_op jit(solution)/shard_map/ppermute | solution.py:256
  23.3 0.5 %shard_map.20 = (f32[256,128]{1,0:T(8,128)S(1)}, f32[256,128]{1,0:T(8,128)S(1)}, f32[256,128]{1,0:T(8,128)S(1)}, bf16[256,128]{1,0:T(8,128)(2,1)S(1)}) custom-call(bf16[8,1024,128]{2,1,0:T(8,128)(2,1)S(1)} %get-tuple-element.13.white), custom_call_target="tpu_custom_call" | custom-call | tf_op jit(solution)/shard_map/pallas_call | solution.py:247
  23.7 0.4 %collective-permute-start.8 = (bf16[256,128]{1,0:T(8,128)(2,1)S(1)}, bf16[256,128]{1,0:T(8,128)(2,1)S(1)}, u32[]{:S(2)}, u32[]{:S(2)}) collective-permute-start(bf16[256,128]{1,0:T(8,128)(2,1)S(1)} %get-tuple-element.20), channel_id=1, source_target_pairs={{0,1},{1,0},{2,3},{3,2},{4,5},{5,4},{6,7},{7,6},{8,9},{9,8},{10,11... | collective-permute-start | bytes 196616 | tf_op jit(solution)/shard_map/ppermute | solution.py:256
  24.1 3.7 %collective-permute-start.3 = (bf16[256,128]{1,0:T(8,128)(2,1)S(1)}, bf16[256,128]{1,0:T(8,128)(2,1)S(1)}, u32[]{:S(2)}, u32[]{:S(2)}) collective-permute-start(bf16[256,128]{1,0:T(8,128)(2,1)S(1)} %get-tuple-element.15), channel_id=1, source_target_pairs={{0,5},{1,4},{2,7},{3,6},{4,1},{5,0},{6,3},{7,2},{8,13},{9,12},{10,... | collective-permute-start | bytes 196616 | tf_op jit(solution)/shard_map/ppermute | solution.py:256
  27.9 0.3 collective-permute-start.4
  28.2 0.0 collective-permute-done.5
  28.2 3.7 %collective-permute-start.6 = (bf16[256,128]{1,0:T(8,128)(2,1)S(1)}, bf16[256,128]{1,0:T(8,128)(2,1)S(1)}, u32[]{:S(2)}, u32[]{:S(2)}) collective-permute-start(bf16[256,128]{1,0:T(8,128)(2,1)S(1)} %get-tuple-element.21), channel_id=1, source_target_pairs={{0,6},{1,7},{2,4},{3,5},{4,2},{5,3},{6,0},{7,1},{8,14},{9,15},{10,... | collective-permute-start | bytes 196616 | tf_op jit(solution)/shard_map/ppermute | solution.py:256
  31.9 0.0 collective-permute-start.7
  31.9 0.0 collective-permute-done.3
  31.9 4.5 %collective-permute-done.4 = bf16[256,128]{1,0:T(8,128)(2,1)S(1)} collective-permute-done((bf16[256,128]{1,0:T(8,128)(2,1)S(1)}, bf16[256,128]{1,0:T(8,128)(2,1)S(1)}, u32[]{:S(2)}, u32[]{:S(2)}) %collective-permute-start.4) | collective-permute-done | bytes 65568 | tf_op jit(solution)/shard_map/ppermute | solution.py:256
  36.5 0.0 collective-permute-done.8
  36.5 0.0 collective-permute-done.6
  36.5 0.4 %collective-permute-done.7 = bf16[256,128]{1,0:T(8,128)(2,1)S(1)} collective-permute-done((bf16[256,128]{1,0:T(8,128)(2,1)S(1)}, bf16[256,128]{1,0:T(8,128)(2,1)S(1)}, u32[]{:S(2)}, u32[]{:S(2)}) %collective-permute-start.7) | collective-permute-done | bytes 65568 | tf_op jit(solution)/shard_map/ppermute | solution.py:256
  36.9 0.7 %add_multiply_fusion = f32[256,128]{1,0:T(8,128)} fusion(bf16[256,128]{1,0:T(8,128)(2,1)S(1)} %collective-permute-done.8, bf16[256,128]{1,0:T(8,128)(2,1)S(1)} %collective-permute-done.7, f32[256,128]{1,0:T(8,128)S(1)} %convert_add_fusion, bf16[256,128]{1,0:T(8,128)(2,1)S(1)} %collective-permute-done.6), kind=kLoop, calls=%fused_computation | loop fusion | flops 229376 | bytes 458752 | tf_op jit(solution)/shard_map/mul | solution.py:270
  (2 shorter events, 0.1 us)
Async XLA Ops:
  0.0 15.1 %collective-permute-start.1 = (bf16[256,1024]{1,0:T(8,128)(2,1)}, bf16[256,1024]{1,0:T(8,128)(2,1)S(1)}, u32[]{:S(2)}, u32[]{:S(2)}) collective-permute-start(bf16[256,1024]{1,0:T(8,128)(2,1)} %refs_0_.3), channel_id=1, source_target_pairs={{0,16},{8,24},{16,0},{24,8},{1,17},{9,25},{17,1},{25,9},{2,18},{10... | collective-permute-start | bytes 1572872 | tf_op jit(solution)/shard_map/ppermute | solution.py:206
  3.0 12.1 %collective-permute-start = (bf16[256,1024]{1,0:T(8,128)(2,1)}, bf16[256,1024]{1,0:T(8,128)(2,1)S(1)}, u32[]{:S(2)}, u32[]{:S(2)}) collective-permute-start(bf16[256,1024]{1,0:T(8,128)(2,1)} %refs_0_.3), channel_id=1, source_target_pairs={{0,8},{8,0},{16,24},{24,16},{1,9},{9,1},{17,25},{25,17},{2,10},{10... | collective-permute-start | bytes 1572872 | tf_op jit(solution)/shard_map/ppermute | solution.py:206
  15.1 1.9 %collective-permute-start.2 = (bf16[256,1024]{1,0:T(8,128)(2,1)S(1)}, bf16[256,1024]{1,0:T(8,128)(2,1)S(1)}, u32[]{:S(2)}, u32[]{:S(2)}) collective-permute-start(bf16[256,1024]{1,0:T(8,128)(2,1)S(1)} %collective-permute-done.1.refs_1_.refs_2_), channel_id=1, source_target_pairs={{0,8},{8,0},{16,24},{24,16},{1,9},{9,1},{17,25},{25,17},{2,10},{10... | collective-permute-start | bytes 1572872 | tf_op jit(solution)/shard_map/ppermute | solution.py:206
  15.1 1.0 %copy-start = (bf16[256,1024]{1,0:T(8,128)(2,1)S(1)}, bf16[256,1024]{1,0:T(8,128)(2,1)}, u32[]{:S(2)}) copy-start(bf16[256,1024]{1,0:T(8,128)(2,1)} %refs_0_.3) | copy-start | bytes 1572868
  16.2 1.0 %copy-start.1 = (bf16[256,1024]{1,0:T(8,128)(2,1)S(1)}, bf16[256,1024]{1,0:T(8,128)(2,1)}, u32[]{:S(2)}) copy-start(bf16[256,1024]{1,0:T(8,128)(2,1)} %refs_0_.3) | copy-start | bytes 1572868
  21.5 6.7 %collective-permute-start.5 = (bf16[512,128]{1,0:T(8,128)(2,1)S(1)}, bf16[512,128]{1,0:T(8,128)(2,1)S(1)}, u32[]{:S(2)}, u32[]{:S(2)}) collective-permute-start(bf16[512,128]{1,0:T(8,128)(2,1)S(1)} %get-tuple-element.18), channel_id=1, source_target_pairs={{0,1},{1,0},{2,3},{3,2},{4,5},{5,4},{6,7},{7,6},{8,9},{9,8},{10,11... | collective-permute-start | bytes 393224 | tf_op jit(solution)/shard_map/ppermute | solution.py:256
  23.7 12.7 %collective-permute-start.8 = (bf16[256,128]{1,0:T(8,128)(2,1)S(1)}, bf16[256,128]{1,0:T(8,128)(2,1)S(1)}, u32[]{:S(2)}, u32[]{:S(2)}) collective-permute-start(bf16[256,128]{1,0:T(8,128)(2,1)S(1)} %get-tuple-element.20), channel_id=1, source_target_pairs={{0,1},{1,0},{2,3},{3,2},{4,5},{5,4},{6,7},{7,6},{8,9},{9,8},{10,11... | collective-permute-start | bytes 196616 | tf_op jit(solution)/shard_map/ppermute | solution.py:256
  24.1 7.8 %collective-permute-start.3 = (bf16[256,128]{1,0:T(8,128)(2,1)S(1)}, bf16[256,128]{1,0:T(8,128)(2,1)S(1)}, u32[]{:S(2)}, u32[]{:S(2)}) collective-permute-start(bf16[256,128]{1,0:T(8,128)(2,1)S(1)} %get-tuple-element.15), channel_id=1, source_target_pairs={{0,5},{1,4},{2,7},{3,6},{4,1},{5,0},{6,3},{7,2},{8,13},{9,12},{10,... | collective-permute-start | bytes 196616 | tf_op jit(solution)/shard_map/ppermute | solution.py:256
  27.9 8.6 %collective-permute-start.4 = (bf16[256,128]{1,0:T(8,128)(2,1)S(1)}, bf16[256,128]{1,0:T(8,128)(2,1)S(1)}, u32[]{:S(2)}, u32[]{:S(2)}) collective-permute-start(bf16[256,128]{1,0:T(8,128)(2,1)S(1)} %get-tuple-element.16), channel_id=1, source_target_pairs={{0,4},{1,5},{2,6},{3,7},{4,0},{5,1},{6,2},{7,3},{8,12},{9,13},{10,... | collective-permute-start | bytes 196616 | tf_op jit(solution)/shard_map/ppermute | solution.py:256
  28.2 8.2 %collective-permute-start.6 = (bf16[256,128]{1,0:T(8,128)(2,1)S(1)}, bf16[256,128]{1,0:T(8,128)(2,1)S(1)}, u32[]{:S(2)}, u32[]{:S(2)}) collective-permute-start(bf16[256,128]{1,0:T(8,128)(2,1)S(1)} %get-tuple-element.21), channel_id=1, source_target_pairs={{0,6},{1,7},{2,4},{3,5},{4,2},{5,3},{6,0},{7,1},{8,14},{9,15},{10,... | collective-permute-start | bytes 196616 | tf_op jit(solution)/shard_map/ppermute | solution.py:256
  31.9 5.0 %collective-permute-start.7 = (bf16[256,128]{1,0:T(8,128)(2,1)S(1)}, bf16[256,128]{1,0:T(8,128)(2,1)S(1)}, u32[]{:S(2)}, u32[]{:S(2)}) collective-permute-start(bf16[256,128]{1,0:T(8,128)(2,1)S(1)} %get-tuple-element.22), channel_id=1, source_target_pairs={{0,2},{1,3},{2,0},{3,1},{4,6},{5,7},{6,4},{7,5},{8,10},{9,11},{10,... | collective-permute-start | bytes 196616 | tf_op jit(solution)/shard_map/ppermute | solution.py:256

commit v3 on v2

--- a/solution.py
+++ b/solution.py
@@ -86,21 +86,20 @@
         panel = [rows[at(first + q), :] for q in range(SUB)]
         near = [lane_gather(row, base + p) for row in panel]
         inside = chunk == p
+        panel = [jnp.where(inside, 0.0, row) for row in panel]
         steps = []
         for q in range(SUB):
-            here = column == first + q
             pivot = broadcast_row(near[q], q)
             inv = 1.0 / pivot
-            step = jnp.where(here, 1.0, panel[q]) * inv
+            lead = jnp.where(column == first + q, 1.0, panel[q])
+            step = lead * inv
             near_step = near[q] * inv
             for k in range(q + 1, SUB):
                 down = broadcast_row(near[q], k)
-                panel[k] = jnp.where(here, 0.0, panel[k]) - down * step
+                panel[k] = panel[k] - down * step
                 near[k] = near[k] - down * near_step
-            steps.append(jnp.where(jnp.logical_and(inside, sub > q), 0.0, step))
-            rows[at(first + q), :] = jnp.where(
-                column < first + q, panel[q], jnp.where(here, 1.0, 0.0)
-            ) * lax.rsqrt(pivot)
+            steps.append(step)
+            rows[at(first + q), :] = jnp.where(chunk > p, 0.0, lead) * lax.rsqrt(pivot)
         for hi in range(p + 1, BW // SUB):
             downs = [lane_gather(row, base + hi) for row in panel]
             for lo in range(SUB):
@@ -111,33 +110,35 @@
                 rows[at(k), :] = row
 
 
-def sums_body(*refs, resumed):
+def sums_body(*refs):
     *grads, sums = refs
-    before = grads.pop(0) if resumed else None
 
     def store(s, value):
-        sums[s] = before[s] + value if resumed else value
+        sums[s] = value
 
     fisher_sums(grads, store)
 
 
-def body(sums_ref, *refs, slots, total, first):
-    grads = refs[:slots]
-    *refs_out, white, packed, rows, inverse = refs[slots:]
-    count, width = grads[0].shape
-    groups = width // LANES
-
+def factor_body(*refs, total):
+    *sums, inverse, packed, rows = refs
+    groups = sums[0].shape[0]
     lane = lax.broadcasted_iota(jnp.int32, (BW, LANES), 1)
     sub = lax.broadcasted_iota(jnp.int32, (BW, LANES), 0)
     unit = jnp.where(sub == lane % BW, 0.1, 0.0)
-
-    def store(s, value):
-        packed[s * BW : (s + 1) * BW, :] = (sums_ref[s] + value) * (1.0 / total) + unit
-
-    fisher_sums(grads[slots // 2 + 1 :: 2], store)
+    for s in range(groups):
+        whole = sums[0][s]
+        for more in sums[1:]:
+            whole = whole + more[s]
+        packed[s * BW : (s + 1) * BW, :] = whole * (1.0 / total) + unit
     to_lanes(packed, rows, groups)
     factor(rows)
     from_lanes(rows, inverse, groups)
+
+
+def body(inverse, *refs, slots, first):
+    grads = refs[:slots]
+    *refs_out, white = refs[slots:]
+    count, width = grads[0].shape
 
     wide = min(2 * LANES, width)
     pairs = wide // LANES
@@ -151,10 +152,12 @@
         matrix = jnp.concatenate(blocks, axis=0)
         high = matrix.astype(jnp.bfloat16)
         rest = (matrix - high.astype(jnp.float32)).astype(jnp.bfloat16)
-        x = jnp.concatenate([g[:, w * wide : (w + 1) * wide] for g in grads], axis=0)
-        out = (times(x, high) + times(x, rest)).astype(jnp.bfloat16)
-        for h in range(pairs):
-            white[w * pairs + h] = out[:, h * LANES : (h + 1) * LANES]
+        both = jnp.concatenate([high, rest], axis=0)
+        for t in range(slots):
+            x = grads[t][:, w * wide : (w + 1) * wide]
+            out = times(jnp.concatenate([x, x], axis=1), both).astype(jnp.bfloat16)
+            for h in range(pairs):
+                white[w * pairs + h, t * count : (t + 1) * count, :] = out[:, h * LANES : (h + 1) * LANES]
 
     products(white, refs_out, first, count)
 
@@ -205,9 +208,9 @@
     def swap(x, bit):
         return lax.ppermute(x, "row", [(i, i ^ bit) for i in range(slots)])
 
-    def sums_of(arrays, resumed):
+    def sums_of(arrays):
         return pl.pallas_call(
-            functools.partial(sums_body, resumed=resumed),
+            sums_body,
             in_specs=[vmem] * len(arrays),
             out_specs=vmem,
             out_shape=jax.ShapeDtypeStruct((groups, BW, LANES), jnp.float32),
@@ -222,8 +225,20 @@
             held[t ^ bit] = swap(held[t], bit)
         bit //= 2
 
-    sums = sums_of([held[t] for t in range(far)], False)
-    sums = sums_of([sums] + [held[t] for t in range(far, slots, 2)], True)
+    sums = [sums_of([held[t] for t in range(far)])]
+    sums.append(sums_of([held[t] for t in range(far, slots, 2)]))
+    sums.append(swap(sums[1], 1))
+    inverse = pl.pallas_call(
+        functools.partial(factor_body, total=total),
+        in_specs=[vmem] * len(sums),
+        out_specs=vmem,
+        out_shape=jax.ShapeDtypeStruct((groups * LANES, LANES), jnp.float32),
+        scratch_shapes=[
+            pltpu.VMEM((groups * BW, LANES), jnp.float32),
+            pltpu.VMEM((BW * SUB, LANES), jnp.float32),
+        ],
+        compiler_params=params,
+    )(*sums)
 
     def results(asked, dtypes):
         return [
@@ -232,18 +247,13 @@
         ]
 
     urgent, *sent, white = pl.pallas_call(
-        functools.partial(body, slots=slots, total=total, first=first),
+        functools.partial(body, slots=slots, first=first),
         in_specs=[vmem] * (slots + 1),
         out_specs=[vmem] * (len(first) + 1),
         out_shape=results(first, [jnp.bfloat16] * len(first))
         + [jax.ShapeDtypeStruct((groups, total, LANES), jnp.bfloat16)],
-        scratch_shapes=[
-            pltpu.VMEM((groups * BW, LANES), jnp.float32),
-            pltpu.VMEM((BW * SUB, LANES), jnp.float32),
-            pltpu.VMEM((groups * LANES, LANES), jnp.float32),
-        ],
         compiler_params=params,
-    )(sums, *[held[t] for t in range(slots)])
+    )(inverse, *[held[t] for t in range(slots)])
     *kept, own, loan = pl.pallas_call(
         functools.partial(rest_body, asked=second, count=count),
         in_specs=[vmem],

time: 37.8 us -> 37.3 us (0.987)
  starting transfers between devices: 12.9 us -> 13.4 us
  waiting for transfers between devices: 17.1 us -> 16.6 us
    ppermute x3 -> x4, starting transfers between devices: 3 us -> 3.58 us  [swap(): return lax.ppermute(x, 'row', [(i, i ^ bit) for i in range(slots)])]
    ppermute x6, waiting for transfers between devices: 4.92 us -> 4.37 us  [exchange(): return lax.ppermute(x, 'col', [(i, i ^ p) for i in range(peers)])]
    pallas_call x3 -> x4, Pallas kernels: 5.12 us -> 4.77 us  [the longest x1 2.21 us: per_device(): pl.pallas_call(functools.partial(factor_body, total=total), in_specs=[vme...]
    ppermute x3 -> x4, waiting for transfers between devices: 12.1 us -> 12.2 us  [swap(): return lax.ppermute(x, 'row', [(i, i ^ bit) for i in range(slots)])]
  transfers between devices with their start and end apart: 9 -> 10, of which waited for: 3 -> 3; matrix products, arithmetic and copies ran while one was open for 0% -> 0% of each run, Pallas kernels for 3% -> 9%
where the time goes in v3:
time: 37.3 us; the launch traced here: 37.1 us
  waiting for transfers between devices  16.6 us (45%)
  starting transfers between devices  13.4 us (36%)
  Pallas kernels  5.24 us (14%)
  local copies, waits for them, and re-layouts  1.05 us (3%)
  other arithmetic  0.74 us (2%)
    ppermute x4, waiting for transfers between devices, swap(): return lax.ppermute(x, 'row', [(i, i ^ bit) for i in range(slots)])  12.2 us
    ppermute x6, starting transfers between devices, exchange(): return lax.ppermute(x, 'col', [(i, i ^ p) for i in range(peers)])  9.83 us
    ppermute x6, waiting for transfers between devices, exchange(): return lax.ppermute(x, 'col', [(i, i ^ p) for i in range(peers)])  4.37 us
    ppermute x4, starting transfers between devices, swap(): return lax.ppermute(x, 'row', [(i, i ^ bit) for i in range(slots)])  3.58 us
    pallas_call x1, Pallas kernels, per_device(): pl.pallas_call(functools.partial(factor_body, total=total), in_specs=[vme...  2.21 us
    pallas_call x1, Pallas kernels, per_device(): pl.pallas_call(functools.partial(body, slots=slots, first=first), in_spec...  1.73 us
    unnamed x4, local copies, waits for them, and re-layouts  1.05 us
    pallas_call x2, Pallas kernels, sums_of(): pl.pallas_call(sums_body, in_specs=[vmem] * len(arrays), out_specs=vmem,...  0.84 us
  transfers between devices with their start and end apart: 10, of which 3 were waited for; matrix products, arithmetic and copies ran while one was open for 0% of the time, Pallas kernels for 9%

profile of v3, /device:TPU:0, one launch (start us, length us, event | category | flops | bytes accessed | tf_op | source)
XLA Modules:
  0.0 37.1 jit_solution(17718097102410957594)
XLA Ops:
  0.0 0.0 copy-start.1
  0.0 3.0 %collective-permute-start.1 = (bf16[256,1024]{1,0:T(8,128)(2,1)}, bf16[256,1024]{1,0:T(8,128)(2,1)S(1)}, u32[]{:S(2)}, u32[]{:S(2)}) collective-permute-start(bf16[256,1024]{1,0:T(8,128)(2,1)} %refs_0_.3), channel_id=1, source_target_pairs={{0,16},{8,24},{16,0},{24,8},{1,17},{9,25},{17,1},{25,9},{2,18},{10... | collective-permute-start | bytes 1572872 | tf_op jit(solution)/shard_map/ppermute | solution.py:209
  3.0 0.0 collective-permute-start
  3.0 12.2 %collective-permute-done.1.refs_0_.refs_2_ = bf16[256,1024]{1,0:T(8,128)(2,1)S(1)} collective-permute-done((bf16[256,1024]{1,0:T(8,128)(2,1)}, bf16[256,1024]{1,0:T(8,128)(2,1)S(1)}, u32[]{:S(2)}, u32[]{:S(2)}) %collective-permute-start.1) | collective-permute-done | bytes 524320 | tf_op jit(solution)/shard_map/ppermute | solution.py:209
  15.2 0.0 collective-permute-start.3
  15.2 0.3 shard_map.18.refs_1_
  15.6 0.6 %collective-permute-start.2 = (f32[8,64,128]{2,1,0:T(8,128)S(1)}, f32[8,64,128]{2,1,0:T(8,128)S(1)}, u32[]{:S(2)}, u32[]{:S(2)}) collective-permute-start(f32[8,64,128]{2,1,0:T(8,128)S(1)} %shard_map.18.refs_1_), channel_id=1, source_target_pairs={{0,8},{8,0},{16,24},{24,16},{1,9},{9,1},{17,25},{25,17},{2,10},{10... | collective-permute-start | bytes 786440 | tf_op jit(solution)/shard_map/ppermute | solution.py:209
  16.1 0.0 collective-permute-done.refs_1_
  16.1 0.0 copy-start
  16.1 1.0 %copy-done = bf16[256,1024]{1,0:T(8,128)(2,1)S(1)} copy-done((bf16[256,1024]{1,0:T(8,128)(2,1)S(1)}, bf16[256,1024]{1,0:T(8,128)(2,1)}, u32[]{:S(2)}) %copy-start) | copy-done | bytes 524312
  17.2 0.5 %shard_map.17.refs_0_ = f32[8,64,128]{2,1,0:T(8,128)S(1)} custom-call(bf16[256,1024]{1,0:T(8,128)(2,1)S(1)} %copy-done, bf16[256,1024]{1,0:T(8,128)(2,1)S(1)} %collective-permute-done.refs_1_), custom_call_target="tpu_custom_call" | custom-call | tf_op jit(solution)/shard_map/pallas_call | solution.py:212
  17.7 0.0 collective-permute-done.2.refs_2_
  17.7 2.2 %shard_map.19.inverse = f32[1024,128]{1,0:T(8,128)S(1)} custom-call(f32[8,64,128]{2,1,0:T(8,128)S(1)} %shard_map.17.refs_0_, f32[8,64,128]{2,1,0:T(8,128)S(1)} %shard_map.18.refs_1_, f32[8,64,128]{2,1,0:T(8,128)S(1)} %collective-permute-done.2.refs_2_), custom_call_target="tpu_custom_call" | custom-call | tf_op jit(solution)/shard_map/pallas_call | solution.py:231
  19.9 0.0 collective-permute-done.3.refs_3_
  19.9 0.0 copy-done.1
  19.9 1.7 %shard_map.20 = (bf16[512,128]{1,0:T(8,128)(2,1)S(1)}, bf16[256,128]{1,0:T(8,128)(2,1)S(1)}, bf16[256,128]{1,0:T(8,128)(2,1)S(1)}, bf16[8,1024,128]{2,1,0:T(8,128)(2,1)S(1)}) custom-call(f32[1024,128]{1,0:T(8,128)S(1)} %shard_map.19.inverse, bf16[256,1024]{1,0:T(8,128)(2,1)S(1)} %copy-done.1, bf16[256,1024]{1,0:T(8,128)(2,1)S(1)} %collective-permute-done.refs_1_, ...), custom_call_target="tpu_custom_call" | custom-call | tf_op jit(solution)/shard_map/pallas_call | solution.py:249
  21.7 1.7 %collective-permute-start.6 = (bf16[512,128]{1,0:T(8,128)(2,1)S(1)}, bf16[512,128]{1,0:T(8,128)(2,1)S(1)}, u32[]{:S(2)}, u32[]{:S(2)}) collective-permute-start(bf16[512,128]{1,0:T(8,128)(2,1)S(1)} %get-tuple-element.18), channel_id=1, source_target_pairs={{0,1},{1,0},{2,3},{3,2},{4,5},{5,4},{6,7},{7,6},{8,9},{9,8},{10,11... | collective-permute-start | bytes 393224 | tf_op jit(solution)/shard_map/ppermute | solution.py:266
  23.4 0.5 %shard_map.21 = (f32[256,128]{1,0:T(8,128)S(1)}, f32[256,128]{1,0:T(8,128)S(1)}, f32[256,128]{1,0:T(8,128)S(1)}, bf16[256,128]{1,0:T(8,128)(2,1)S(1)}) custom-call(bf16[8,1024,128]{2,1,0:T(8,128)(2,1)S(1)} %get-tuple-element.13.white), custom_call_target="tpu_custom_call" | custom-call | tf_op jit(solution)/shard_map/pallas_call | solution.py:257
  23.8 0.5 %collective-permute-start.9 = (bf16[256,128]{1,0:T(8,128)(2,1)S(1)}, bf16[256,128]{1,0:T(8,128)(2,1)S(1)}, u32[]{:S(2)}, u32[]{:S(2)}) collective-permute-start(bf16[256,128]{1,0:T(8,128)(2,1)S(1)} %get-tuple-element.20), channel_id=1, source_target_pairs={{0,1},{1,0},{2,3},{3,2},{4,5},{5,4},{6,7},{7,6},{8,9},{9,8},{10,11... | collective-permute-start | bytes 196616 | tf_op jit(solution)/shard_map/ppermute | solution.py:266
  24.3 3.7 %collective-permute-start.4 = (bf16[256,128]{1,0:T(8,128)(2,1)S(1)}, bf16[256,128]{1,0:T(8,128)(2,1)S(1)}, u32[]{:S(2)}, u32[]{:S(2)}) collective-permute-start(bf16[256,128]{1,0:T(8,128)(2,1)S(1)} %get-tuple-element.15), channel_id=1, source_target_pairs={{0,5},{1,4},{2,7},{3,6},{4,1},{5,0},{6,3},{7,2},{8,13},{9,12},{10,... | collective-permute-start | bytes 196616 | tf_op jit(solution)/shard_map/ppermute | solution.py:266
  28.0 0.3 collective-permute-start.5
  28.3 0.0 collective-permute-done.6
  28.3 3.7 %collective-permute-start.7 = (bf16[256,128]{1,0:T(8,128)(2,1)S(1)}, bf16[256,128]{1,0:T(8,128)(2,1)S(1)}, u32[]{:S(2)}, u32[]{:S(2)}) collective-permute-start(bf16[256,128]{1,0:T(8,128)(2,1)S(1)} %get-tuple-element.21), channel_id=1, source_target_pairs={{0,6},{1,7},{2,4},{3,5},{4,2},{5,3},{6,0},{7,1},{8,14},{9,15},{10,... | collective-permute-start | bytes 196616 | tf_op jit(solution)/shard_map/ppermute | solution.py:266
  32.0 0.0 collective-permute-start.8
  32.0 0.0 collective-permute-done.4
  32.0 3.9 %collective-permute-done.5 = bf16[256,128]{1,0:T(8,128)(2,1)S(1)} collective-permute-done((bf16[256,128]{1,0:T(8,128)(2,1)S(1)}, bf16[256,128]{1,0:T(8,128)(2,1)S(1)}, u32[]{:S(2)}, u32[]{:S(2)}) %collective-permute-start.5) | collective-permute-done | bytes 65568 | tf_op jit(solution)/shard_map/ppermute | solution.py:266
  35.9 0.0 collective-permute-done.9
  35.9 0.0 collective-permute-done.7
  35.9 0.5 %collective-permute-done.8 = bf16[256,128]{1,0:T(8,128)(2,1)S(1)} collective-permute-done((bf16[256,128]{1,0:T(8,128)(2,1)S(1)}, bf16[256,128]{1,0:T(8,128)(2,1)S(1)}, u32[]{:S(2)}, u32[]{:S(2)}) %collective-permute-start.8) | collective-permute-done | bytes 65568 | tf_op jit(solution)/shard_map/ppermute | solution.py:266
  36.4 0.7 %add_multiply_fusion = f32[256,128]{1,0:T(8,128)} fusion(bf16[256,128]{1,0:T(8,128)(2,1)S(1)} %collective-permute-done.9, bf16[256,128]{1,0:T(8,128)(2,1)S(1)} %collective-permute-done.8, f32[256,128]{1,0:T(8,128)S(1)} %convert_add_fusion, bf16[256,128]{1,0:T(8,128)(2,1)S(1)} %collective-permute-done.7), kind=kLoop, calls=%fused_computation | loop fusion | flops 229376 | bytes 458752 | tf_op jit(solution)/shard_map/mul | solution.py:280
  (2 shorter events, 0.1 us)
Async XLA Ops:
  0.0 19.9 %copy-start.1 = (bf16[256,1024]{1,0:T(8,128)(2,1)S(1)}, bf16[256,1024]{1,0:T(8,128)(2,1)}, u32[]{:S(2)}) copy-start(bf16[256,1024]{1,0:T(8,128)(2,1)} %refs_0_.3) | copy-start | bytes 1572868
  0.0 15.2 %collective-permute-start.1 = (bf16[256,1024]{1,0:T(8,128)(2,1)}, bf16[256,1024]{1,0:T(8,128)(2,1)S(1)}, u32[]{:S(2)}, u32[]{:S(2)}) collective-permute-start(bf16[256,1024]{1,0:T(8,128)(2,1)} %refs_0_.3), channel_id=1, source_target_pairs={{0,16},{8,24},{16,0},{24,8},{1,17},{9,25},{17,1},{25,9},{2,18},{10... | collective-permute-start | bytes 1572872 | tf_op jit(solution)/shard_map/ppermute | solution.py:209
  3.0 13.1 %collective-permute-start = (bf16[256,1024]{1,0:T(8,128)(2,1)}, bf16[256,1024]{1,0:T(8,128)(2,1)S(1)}, u32[]{:S(2)}, u32[]{:S(2)}) collective-permute-start(bf16[256,1024]{1,0:T(8,128)(2,1)} %refs_0_.3), channel_id=1, source_target_pairs={{0,8},{8,0},{16,24},{24,16},{1,9},{9,1},{17,25},{25,17},{2,10},{10... | collective-permute-start | bytes 1572872 | tf_op jit(solution)/shard_map/ppermute | solution.py:209
  15.2 4.7 %collective-permute-start.3 = (bf16[256,1024]{1,0:T(8,128)(2,1)S(1)}, bf16[256,1024]{1,0:T(8,128)(2,1)S(1)}, u32[]{:S(2)}, u32[]{:S(2)}) collective-permute-start(bf16[256,1024]{1,0:T(8,128)(2,1)S(1)} %collective-permute-done.1.refs_0_.refs_2_), channel_id=1, source_target_pairs={{0,8},{8,0},{16,24},{24,16},{1,9},{9,1},{17,25},{25,17},{2,10},{10... | collective-permute-start | bytes 1572872 | tf_op jit(solution)/shard_map/ppermute | solution.py:209
  15.6 2.1 %collective-permute-start.2 = (f32[8,64,128]{2,1,0:T(8,128)S(1)}, f32[8,64,128]{2,1,0:T(8,128)S(1)}, u32[]{:S(2)}, u32[]{:S(2)}) collective-permute-start(f32[8,64,128]{2,1,0:T(8,128)S(1)} %shard_map.18.refs_1_), channel_id=1, source_target_pairs={{0,8},{8,0},{16,24},{24,16},{1,9},{9,1},{17,25},{25,17},{2,10},{10... | collective-permute-start | bytes 786440 | tf_op jit(solution)/shard_map/ppermute | solution.py:209
  16.1 1.0 %copy-start = (bf16[256,1024]{1,0:T(8,128)(2,1)S(1)}, bf16[256,1024]{1,0:T(8,128)(2,1)}, u32[]{:S(2)}) copy-start(bf16[256,1024]{1,0:T(8,128)(2,1)} %refs_0_.3) | copy-start | bytes 1572868
  21.7 6.6 %collective-permute-start.6 = (bf16[512,128]{1,0:T(8,128)(2,1)S(1)}, bf16[512,128]{1,0:T(8,128)(2,1)S(1)}, u32[]{:S(2)}, u32[]{:S(2)}) collective-permute-start(bf16[512,128]{1,0:T(8,128)(2,1)S(1)} %get-tuple-element.18), channel_id=1, source_target_pairs={{0,1},{1,0},{2,3},{3,2},{4,5},{5,4},{6,7},{7,6},{8,9},{9,8},{10,11... | collective-permute-start | bytes 393224 | tf_op jit(solution)/shard_map/ppermute | solution.py:266
  23.8 12.1 %collective-permute-start.9 = (bf16[256,128]{1,0:T(8,128)(2,1)S(1)}, bf16[256,128]{1,0:T(8,128)(2,1)S(1)}, u32[]{:S(2)}, u32[]{:S(2)}) collective-permute-start(bf16[256,128]{1,0:T(8,128)(2,1)S(1)} %get-tuple-element.20), channel_id=1, source_target_pairs={{0,1},{1,0},{2,3},{3,2},{4,5},{5,4},{6,7},{7,6},{8,9},{9,8},{10,11... | collective-permute-start | bytes 196616 | tf_op jit(solution)/shard_map/ppermute | solution.py:266
  24.3 7.7 %collective-permute-start.4 = (bf16[256,128]{1,0:T(8,128)(2,1)S(1)}, bf16[256,128]{1,0:T(8,128)(2,1)S(1)}, u32[]{:S(2)}, u32[]{:S(2)}) collective-permute-start(bf16[256,128]{1,0:T(8,128)(2,1)S(1)} %get-tuple-element.15), channel_id=1, source_target_pairs={{0,5},{1,4},{2,7},{3,6},{4,1},{5,0},{6,3},{7,2},{8,13},{9,12},{10,... | collective-permute-start | bytes 196616 | tf_op jit(solution)/shard_map/ppermute | solution.py:266
  28.0 7.9 %collective-permute-start.5 = (bf16[256,128]{1,0:T(8,128)(2,1)S(1)}, bf16[256,128]{1,0:T(8,128)(2,1)S(1)}, u32[]{:S(2)}, u32[]{:S(2)}) collective-permute-start(bf16[256,128]{1,0:T(8,128)(2,1)S(1)} %get-tuple-element.16), channel_id=1, source_target_pairs={{0,4},{1,5},{2,6},{3,7},{4,0},{5,1},{6,2},{7,3},{8,12},{9,13},{10,... | collective-permute-start | bytes 196616 | tf_op jit(solution)/shard_map/ppermute | solution.py:266
  28.3 7.6 %collective-permute-start.7 = (bf16[256,128]{1,0:T(8,128)(2,1)S(1)}, bf16[256,128]{1,0:T(8,128)(2,1)S(1)}, u32[]{:S(2)}, u32[]{:S(2)}) collective-permute-start(bf16[256,128]{1,0:T(8,128)(2,1)S(1)} %get-tuple-element.21), channel_id=1, source_target_pairs={{0,6},{1,7},{2,4},{3,5},{4,2},{5,3},{6,0},{7,1},{8,14},{9,15},{10,... | collective-permute-start | bytes 196616 | tf_op jit(solution)/shard_map/ppermute | solution.py:266
  32.0 4.4 %collective-permute-start.8 = (bf16[256,128]{1,0:T(8,128)(2,1)S(1)}, bf16[256,128]{1,0:T(8,128)(2,1)S(1)}, u32[]{:S(2)}, u32[]{:S(2)}) collective-permute-start(bf16[256,128]{1,0:T(8,128)(2,1)S(1)} %get-tuple-element.22), channel_id=1, source_target_pairs={{0,2},{1,3},{2,0},{3,1},{4,6},{5,7},{6,4},{7,5},{8,10},{9,11},{10,... | collective-permute-start | bytes 196616 | tf_op jit(solution)/shard_map/ppermute | solution.py:266

commit v4 on v3

--- a/solution.py
+++ b/solution.py
@@ -191,6 +191,14 @@
     products(white, outs, asked, count)
 
 
+def total_body(*refs, scale):
+    *parts, out = refs
+    whole = parts[0][...]
+    for part in parts[1:]:
+        whole = whole + part[...].astype(jnp.float32)
+    out[...] = whole * scale
+
+
 def per_device(grads):
     slots = lax.axis_size("row")
     peers = lax.axis_size("col")
@@ -274,10 +282,14 @@
     kernel = own
     for part in got[: len(straight)]:
         kernel = kernel + part.astype(jnp.float32)
-    kernel = lax.optimization_barrier(kernel)
-    for part in [*got[len(straight) :], loan]:
-        kernel = kernel + part.astype(jnp.float32)
-    return kernel * (width * peers) ** (-0.5)
+    late = [*got[len(straight) :], loan]
+    return pl.pallas_call(
+        functools.partial(total_body, scale=(width * peers) ** (-0.5)),
+        in_specs=[vmem] * (len(late) + 1),
+        out_specs=vmem,
+        out_shape=jax.ShapeDtypeStruct((count, block), jnp.float32),
+        compiler_params=params,
+    )(kernel, *late)
 
 
 def solution(mesh):

time: 37.3 us -> 37 us (level)
  waiting for transfers between devices: 16.6 us -> 15.9 us
  other arithmetic: 0.74 us -> 0.05 us
  Pallas kernels: 5.24 us -> 5.93 us
  starting transfers between devices: 13.4 us -> 13.9 us
    ppermute x6, waiting for transfers between devices: 4.37 us -> 3.65 us  [exchange(): return lax.ppermute(x, 'col', [(i, i ^ p) for i in range(peers)])]
    mul x1 -> x0, other arithmetic: 0.69 us -> none  [per_device(): return kernel * (width * peers) ** (-0.5)]
    pallas_call x0 -> x1, Pallas kernels: none -> 0.69 us  [per_device(): pl.pallas_call(functools.partial(total_body, scale=(width * peers) ** (-0...]
    ppermute x6, starting transfers between devices: 9.83 us -> 10.3 us  [exchange(): return lax.ppermute(x, 'col', [(i, i ^ p) for i in range(peers)])]
  transfers between devices with their start and end apart: 10 -> 10, of which waited for: 3 -> 3; matrix products, arithmetic and copies ran while one was open for 0% -> 0% of each run, Pallas kernels for 9% -> 10%
where the time goes in v4:
time: 37 us; the launch traced here: 36.8 us
  waiting for transfers between devices  15.9 us (43%)
  starting transfers between devices  13.9 us (38%)
  Pallas kernels  5.93 us (16%)
  local copies, waits for them, and re-layouts  1.05 us (3%)
    ppermute x4, waiting for transfers between devices, swap(): return lax.ppermute(x, 'row', [(i, i ^ bit) for i in range(slots)])  12.2 us
    ppermute x6, starting transfers between devices, exchange(): return lax.ppermute(x, 'col', [(i, i ^ p) for i in range(peers)])  10.3 us
    ppermute x6, waiting for transfers between devices, exchange(): return lax.ppermute(x, 'col', [(i, i ^ p) for i in range(peers)])  3.65 us
    ppermute x4, starting transfers between devices, swap(): return lax.ppermute(x, 'row', [(i, i ^ bit) for i in range(slots)])  3.58 us
    pallas_call x1, Pallas kernels, per_device(): pl.pallas_call(functools.partial(factor_body, total=total), in_specs=[vme...  2.21 us
    pallas_call x1, Pallas kernels, per_device(): pl.pallas_call(functools.partial(body, slots=slots, first=first), in_spec...  1.73 us
    unnamed x4, local copies, waits for them, and re-layouts  1.05 us
    pallas_call x2, Pallas kernels, sums_of(): pl.pallas_call(sums_body, in_specs=[vmem] * len(arrays), out_specs=vmem,...  0.84 us
  transfers between devices with their start and end apart: 10, of which 3 were waited for; matrix products, arithmetic and copies ran while one was open for 0% of the time, Pallas kernels for 10%

profile of v4, /device:TPU:0, one launch (start us, length us, event | category | flops | bytes accessed | tf_op | source)
XLA Modules:
  0.0 36.8 jit_solution(2138012451369775495)
XLA Ops:
  0.0 0.0 copy-start.1
  0.0 3.0 %collective-permute-start.1 = (bf16[256,1024]{1,0:T(8,128)(2,1)}, bf16[256,1024]{1,0:T(8,128)(2,1)S(1)}, u32[]{:S(2)}, u32[]{:S(2)}) collective-permute-start(bf16[256,1024]{1,0:T(8,128)(2,1)} %refs_0_.3), channel_id=1, source_target_pairs={{0,16},{8,24},{16,0},{24,8},{1,17},{9,25},{17,1},{25,9},{2,18},{10... | collective-permute-start | bytes 1572872 | tf_op jit(solution)/shard_map/ppermute | solution.py:217
  3.0 0.0 collective-permute-start
  3.0 12.2 %collective-permute-done.1.refs_0_.refs_2_ = bf16[256,1024]{1,0:T(8,128)(2,1)S(1)} collective-permute-done((bf16[256,1024]{1,0:T(8,128)(2,1)}, bf16[256,1024]{1,0:T(8,128)(2,1)S(1)}, u32[]{:S(2)}, u32[]{:S(2)}) %collective-permute-start.1) | collective-permute-done | bytes 524320 | tf_op jit(solution)/shard_map/ppermute | solution.py:217
  15.2 0.0 collective-permute-start.3
  15.2 0.3 shard_map.18.refs_1_
  15.6 0.6 %collective-permute-start.2 = (f32[8,64,128]{2,1,0:T(8,128)S(1)}, f32[8,64,128]{2,1,0:T(8,128)S(1)}, u32[]{:S(2)}, u32[]{:S(2)}) collective-permute-start(f32[8,64,128]{2,1,0:T(8,128)S(1)} %shard_map.18.refs_1_), channel_id=1, source_target_pairs={{0,8},{8,0},{16,24},{24,16},{1,9},{9,1},{17,25},{25,17},{2,10},{10... | collective-permute-start | bytes 786440 | tf_op jit(solution)/shard_map/ppermute | solution.py:217
  16.1 0.0 collective-permute-done.refs_1_
  16.1 0.0 copy-start
  16.1 1.0 %copy-done = bf16[256,1024]{1,0:T(8,128)(2,1)S(1)} copy-done((bf16[256,1024]{1,0:T(8,128)(2,1)S(1)}, bf16[256,1024]{1,0:T(8,128)(2,1)}, u32[]{:S(2)}) %copy-start) | copy-done | bytes 524312
  17.2 0.5 %shard_map.17.refs_0_ = f32[8,64,128]{2,1,0:T(8,128)S(1)} custom-call(bf16[256,1024]{1,0:T(8,128)(2,1)S(1)} %copy-done, bf16[256,1024]{1,0:T(8,128)(2,1)S(1)} %collective-permute-done.refs_1_), custom_call_target="tpu_custom_call" | custom-call | tf_op jit(solution)/shard_map/pallas_call | solution.py:220
  17.7 0.0 collective-permute-done.2.refs_2_
  17.7 2.2 %shard_map.19.inverse = f32[1024,128]{1,0:T(8,128)S(1)} custom-call(f32[8,64,128]{2,1,0:T(8,128)S(1)} %shard_map.17.refs_0_, f32[8,64,128]{2,1,0:T(8,128)S(1)} %shard_map.18.refs_1_, f32[8,64,128]{2,1,0:T(8,128)S(1)} %collective-permute-done.2.refs_2_), custom_call_target="tpu_custom_call" | custom-call | tf_op jit(solution)/shard_map/pallas_call | solution.py:239
  19.9 0.0 collective-permute-done.3.refs_3_
  19.9 0.0 copy-done.1
  19.9 1.7 %shard_map.20 = (bf16[512,128]{1,0:T(8,128)(2,1)S(1)}, bf16[256,128]{1,0:T(8,128)(2,1)S(1)}, bf16[256,128]{1,0:T(8,128)(2,1)S(1)}, bf16[8,1024,128]{2,1,0:T(8,128)(2,1)S(1)}) custom-call(f32[1024,128]{1,0:T(8,128)S(1)} %shard_map.19.inverse, bf16[256,1024]{1,0:T(8,128)(2,1)S(1)} %copy-done.1, bf16[256,1024]{1,0:T(8,128)(2,1)S(1)} %collective-permute-done.refs_1_, ...), custom_call_target="tpu_custom_call" | custom-call | tf_op jit(solution)/shard_map/pallas_call | solution.py:257
  21.7 1.7 %collective-permute-start.6 = (bf16[512,128]{1,0:T(8,128)(2,1)S(1)}, bf16[512,128]{1,0:T(8,128)(2,1)S(1)}, u32[]{:S(2)}, u32[]{:S(2)}) collective-permute-start(bf16[512,128]{1,0:T(8,128)(2,1)S(1)} %get-tuple-element.18), channel_id=1, source_target_pairs={{0,1},{1,0},{2,3},{3,2},{4,5},{5,4},{6,7},{7,6},{8,9},{9,8},{10,11... | collective-permute-start | bytes 393224 | tf_op jit(solution)/shard_map/ppermute | solution.py:274
  23.4 0.5 %shard_map.21 = (f32[256,128]{1,0:T(8,128)S(1)}, f32[256,128]{1,0:T(8,128)S(1)}, f32[256,128]{1,0:T(8,128)S(1)}, bf16[256,128]{1,0:T(8,128)(2,1)S(1)}) custom-call(bf16[8,1024,128]{2,1,0:T(8,128)(2,1)S(1)} %get-tuple-element.13.white), custom_call_target="tpu_custom_call" | custom-call | tf_op jit(solution)/shard_map/pallas_call | solution.py:265
  23.8 0.5 %collective-permute-start.9 = (bf16[256,128]{1,0:T(8,128)(2,1)S(1)}, bf16[256,128]{1,0:T(8,128)(2,1)S(1)}, u32[]{:S(2)}, u32[]{:S(2)}) collective-permute-start(bf16[256,128]{1,0:T(8,128)(2,1)S(1)} %get-tuple-element.20), channel_id=1, source_target_pairs={{0,1},{1,0},{2,3},{3,2},{4,5},{5,4},{6,7},{7,6},{8,9},{9,8},{10,11... | collective-permute-start | bytes 196616 | tf_op jit(solution)/shard_map/ppermute | solution.py:274
  24.3 3.7 %collective-permute-start.4 = (bf16[256,128]{1,0:T(8,128)(2,1)S(1)}, bf16[256,128]{1,0:T(8,128)(2,1)S(1)}, u32[]{:S(2)}, u32[]{:S(2)}) collective-permute-start(bf16[256,128]{1,0:T(8,128)(2,1)S(1)} %get-tuple-element.15), channel_id=1, source_target_pairs={{0,5},{1,4},{2,7},{3,6},{4,1},{5,0},{6,3},{7,2},{8,13},{9,12},{10,... | collective-permute-start | bytes 196616 | tf_op jit(solution)/shard_map/ppermute | solution.py:274
  28.0 0.3 collective-permute-start.5
  28.3 0.0 collective-permute-done.6
  28.3 1.6 %collective-permute-start.8 = (bf16[256,128]{1,0:T(8,128)(2,1)S(1)}, bf16[256,128]{1,0:T(8,128)(2,1)S(1)}, u32[]{:S(2)}, u32[]{:S(2)}) collective-permute-start(bf16[256,128]{1,0:T(8,128)(2,1)S(1)} %get-tuple-element.21), channel_id=1, source_target_pairs={{0,2},{1,3},{2,0},{3,1},{4,6},{5,7},{6,4},{7,5},{8,10},{9,11},{10,... | collective-permute-start | bytes 196616 | tf_op jit(solution)/shard_map/ppermute | solution.py:274
  30.0 2.5 %collective-permute-start.7 = (bf16[256,128]{1,0:T(8,128)(2,1)S(1)}, bf16[256,128]{1,0:T(8,128)(2,1)S(1)}, u32[]{:S(2)}, u32[]{:S(2)}) collective-permute-start(bf16[256,128]{1,0:T(8,128)(2,1)S(1)} %get-tuple-element.22), channel_id=1, source_target_pairs={{0,6},{1,7},{2,4},{3,5},{4,2},{5,3},{6,0},{7,1},{8,14},{9,15},{10,... | collective-permute-start | bytes 196616 | tf_op jit(solution)/shard_map/ppermute | solution.py:274
  32.5 0.0 collective-permute-done.4
  32.5 2.8 %collective-permute-done.5 = bf16[256,128]{1,0:T(8,128)(2,1)S(1)} collective-permute-done((bf16[256,128]{1,0:T(8,128)(2,1)S(1)}, bf16[256,128]{1,0:T(8,128)(2,1)S(1)}, u32[]{:S(2)}, u32[]{:S(2)}) %collective-permute-start.5) | collective-permute-done | bytes 65568 | tf_op jit(solution)/shard_map/ppermute | solution.py:274
  35.3 0.0 collective-permute-done.9.refs_3_
  35.3 0.0 collective-permute-done.8.refs_2_
  35.3 0.8 %collective-permute-done.7.refs_1_ = bf16[256,128]{1,0:T(8,128)(2,1)S(1)} collective-permute-done((bf16[256,128]{1,0:T(8,128)(2,1)S(1)}, bf16[256,128]{1,0:T(8,128)(2,1)S(1)}, u32[]{:S(2)}, u32[]{:S(2)}) %collective-permute-start.7) | collective-permute-done | bytes 65568 | tf_op jit(solution)/shard_map/ppermute | solution.py:274
  36.1 0.7 %shard_map.22 = f32[256,128]{1,0:T(8,128)} custom-call(f32[256,128]{1,0:T(8,128)S(1)} %convert_add_fusion.refs_0_, bf16[256,128]{1,0:T(8,128)(2,1)S(1)} %collective-permute-done.7.refs_1_, bf16[256,128]{1,0:T(8,128)(2,1)S(1)} %collective-permute-done.8.refs_2_, bf16[256,128]{1,0:T(8,128)(2,1)S(1)} %collective-permute-done.9.refs_3_), custom_call_target="tpu_custom_call" | custom-call | tf_op jit(solution)/shard_map/pallas_call | solution.py:286
  (2 shorter events, 0.1 us)
Async XLA Ops:
  0.0 19.9 %copy-start.1 = (bf16[256,1024]{1,0:T(8,128)(2,1)S(1)}, bf16[256,1024]{1,0:T(8,128)(2,1)}, u32[]{:S(2)}) copy-start(bf16[256,1024]{1,0:T(8,128)(2,1)} %refs_0_.3) | copy-start | bytes 1572868
  0.0 15.2 %collective-permute-start.1 = (bf16[256,1024]{1,0:T(8,128)(2,1)}, bf16[256,1024]{1,0:T(8,128)(2,1)S(1)}, u32[]{:S(2)}, u32[]{:S(2)}) collective-permute-start(bf16[256,1024]{1,0:T(8,128)(2,1)} %refs_0_.3), channel_id=1, source_target_pairs={{0,16},{8,24},{16,0},{24,8},{1,17},{9,25},{17,1},{25,9},{2,18},{10... | collective-permute-start | bytes 1572872 | tf_op jit(solution)/shard_map/ppermute | solution.py:217
  3.0 13.1 %collective-permute-start = (bf16[256,1024]{1,0:T(8,128)(2,1)}, bf16[256,1024]{1,0:T(8,128)(2,1)S(1)}, u32[]{:S(2)}, u32[]{:S(2)}) collective-permute-start(bf16[256,1024]{1,0:T(8,128)(2,1)} %refs_0_.3), channel_id=1, source_target_pairs={{0,8},{8,0},{16,24},{24,16},{1,9},{9,1},{17,25},{25,17},{2,10},{10... | collective-permute-start | bytes 1572872 | tf_op jit(solution)/shard_map/ppermute | solution.py:217
  15.2 4.7 %collective-permute-start.3 = (bf16[256,1024]{1,0:T(8,128)(2,1)S(1)}, bf16[256,1024]{1,0:T(8,128)(2,1)S(1)}, u32[]{:S(2)}, u32[]{:S(2)}) collective-permute-start(bf16[256,1024]{1,0:T(8,128)(2,1)S(1)} %collective-permute-done.1.refs_0_.refs_2_), channel_id=1, source_target_pairs={{0,8},{8,0},{16,24},{24,16},{1,9},{9,1},{17,25},{25,17},{2,10},{10... | collective-permute-start | bytes 1572872 | tf_op jit(solution)/shard_map/ppermute | solution.py:217
  15.6 2.1 %collective-permute-start.2 = (f32[8,64,128]{2,1,0:T(8,128)S(1)}, f32[8,64,128]{2,1,0:T(8,128)S(1)}, u32[]{:S(2)}, u32[]{:S(2)}) collective-permute-start(f32[8,64,128]{2,1,0:T(8,128)S(1)} %shard_map.18.refs_1_), channel_id=1, source_target_pairs={{0,8},{8,0},{16,24},{24,16},{1,9},{9,1},{17,25},{25,17},{2,10},{10... | collective-permute-start | bytes 786440 | tf_op jit(solution)/shard_map/ppermute | solution.py:217
  16.1 1.0 %copy-start = (bf16[256,1024]{1,0:T(8,128)(2,1)S(1)}, bf16[256,1024]{1,0:T(8,128)(2,1)}, u32[]{:S(2)}) copy-start(bf16[256,1024]{1,0:T(8,128)(2,1)} %refs_0_.3) | copy-start | bytes 1572868
  21.7 6.6 %collective-permute-start.6 = (bf16[512,128]{1,0:T(8,128)(2,1)S(1)}, bf16[512,128]{1,0:T(8,128)(2,1)S(1)}, u32[]{:S(2)}, u32[]{:S(2)}) collective-permute-start(bf16[512,128]{1,0:T(8,128)(2,1)S(1)} %get-tuple-element.18), channel_id=1, source_target_pairs={{0,1},{1,0},{2,3},{3,2},{4,5},{5,4},{6,7},{7,6},{8,9},{9,8},{10,11... | collective-permute-start | bytes 393224 | tf_op jit(solution)/shard_map/ppermute | solution.py:274
  23.8 11.5 %collective-permute-start.9 = (bf16[256,128]{1,0:T(8,128)(2,1)S(1)}, bf16[256,128]{1,0:T(8,128)(2,1)S(1)}, u32[]{:S(2)}, u32[]{:S(2)}) collective-permute-start(bf16[256,128]{1,0:T(8,128)(2,1)S(1)} %get-tuple-element.20), channel_id=1, source_target_pairs={{0,1},{1,0},{2,3},{3,2},{4,5},{5,4},{6,7},{7,6},{8,9},{9,8},{10,11... | collective-permute-start | bytes 196616 | tf_op jit(solution)/shard_map/ppermute | solution.py:274
  24.3 8.2 %collective-permute-start.4 = (bf16[256,128]{1,0:T(8,128)(2,1)S(1)}, bf16[256,128]{1,0:T(8,128)(2,1)S(1)}, u32[]{:S(2)}, u32[]{:S(2)}) collective-permute-start(bf16[256,128]{1,0:T(8,128)(2,1)S(1)} %get-tuple-element.15), channel_id=1, source_target_pairs={{0,5},{1,4},{2,7},{3,6},{4,1},{5,0},{6,3},{7,2},{8,13},{9,12},{10,... | collective-permute-start | bytes 196616 | tf_op jit(solution)/shard_map/ppermute | solution.py:274
  28.0 7.3 %collective-permute-start.5 = (bf16[256,128]{1,0:T(8,128)(2,1)S(1)}, bf16[256,128]{1,0:T(8,128)(2,1)S(1)}, u32[]{:S(2)}, u32[]{:S(2)}) collective-permute-start(bf16[256,128]{1,0:T(8,128)(2,1)S(1)} %get-tuple-element.16), channel_id=1, source_target_pairs={{0,4},{1,5},{2,6},{3,7},{4,0},{5,1},{6,2},{7,3},{8,12},{9,13},{10,... | collective-permute-start | bytes 196616 | tf_op jit(solution)/shard_map/ppermute | solution.py:274
  28.3 7.0 %collective-permute-start.8 = (bf16[256,128]{1,0:T(8,128)(2,1)S(1)}, bf16[256,128]{1,0:T(8,128)(2,1)S(1)}, u32[]{:S(2)}, u32[]{:S(2)}) collective-permute-start(bf16[256,128]{1,0:T(8,128)(2,1)S(1)} %get-tuple-element.21), channel_id=1, source_target_pairs={{0,2},{1,3},{2,0},{3,1},{4,6},{5,7},{6,4},{7,5},{8,10},{9,11},{10,... | collective-permute-start | bytes 196616 | tf_op jit(solution)/shard_map/ppermute | solution.py:274
  30.0 6.2 %collective-permute-start.7 = (bf16[256,128]{1,0:T(8,128)(2,1)S(1)}, bf16[256,128]{1,0:T(8,128)(2,1)S(1)}, u32[]{:S(2)}, u32[]{:S(2)}) collective-permute-start(bf16[256,128]{1,0:T(8,128)(2,1)S(1)} %get-tuple-element.22), channel_id=1, source_target_pairs={{0,6},{1,7},{2,4},{3,5},{4,2},{5,3},{6,0},{7,1},{8,14},{9,15},{10,... | collective-permute-start | bytes 196616 | tf_op jit(solution)/shard_map/ppermute | solution.py:274
